TPU v7x, 128 devices: a whole 4x4x4 slice. The times are simulated.
128 devices in a mesh: subj: 8 (over z_lo, y), gz: 16 (over x, z_hi, core).
Axes of the slice: x: 4, y: 4, z: 4 (z_hi: 2, z_lo: 2; z = z_hi * 2 + z_lo), core: 2. Of those that a mesh axis runs over, the one named last changes fastest.
Arguments:
- warped: float32 [8, 512, 64, 256], P('subj', 'gz'), may hold values from -12 to 12
Outputs:
- force: float32 [8, 3, 512, 64, 256], P('subj', None, 'gz')
- template: float32 [512, 64, 256], P('gz')
- loss: float32 [8], P('subj')
All inputs are finite; a program needn't handle non-finite values.
Results may differ from a plain program's by a relative error of at most 0.0001.
Values sent between devices are 32-bit elements; how exact they have to be, the bound alone decides.
No kernel may reach another device: no remote copies, remote signals or barrier semaphores. Data moves between devices by JAX's collectives and lax.ppermute only.
A program may use at most 128 MiB of HBM per device.

v0:
```python
import math

import jax
import jax.numpy as jnp
from jax import lax
from jax.sharding import PartitionSpec as P

BOX_R = 4
GAUSS_R = 3


epsilon = 1e-05


def padded_2(array, sides, width):
    for axis, dim in sides:
        size, length = (lax.axis_size(axis), array.shape[dim])
        up = [(i, (i + 1) % size) for i in range(size - 1)]
        down = [(j, i) for i, j in up]
        last = lax.slice_in_dim(array, length - width, length, axis=dim)
        first = lax.slice_in_dim(array, 0, width, axis=dim)
        before = lax.ppermute(last, axis, up)
        after = lax.ppermute(first, axis, down)
        array = jnp.concatenate([before, array, after], axis=dim)
    return array


def shifted_sum(padded, along, planes_out, window_span):
    running = lax.slice_in_dim(padded, 0, planes_out, axis=along)
    for offset in range(1, window_span):
        running = running + lax.slice_in_dim(padded, offset, offset + planes_out, axis=along)
    return running


def window_mean(volume):
    window_span = 2 * BOX_R + 1
    planes_out = volume.shape[0] - 2 * BOX_R
    running = shifted_sum(volume, 0, planes_out, window_span)
    running = shifted_sum(
        jnp.pad(running, ((0, 0), (BOX_R, BOX_R), (0, 0))), 1, volume.shape[1], window_span
    )
    running = shifted_sum(
        jnp.pad(running, ((0, 0), (0, 0), (BOX_R, BOX_R))), 2, volume.shape[2], window_span
    )
    return running / float(window_span**3)


def local_force(moving, target):
    planes_out = moving.shape[0] - 2 * BOX_R
    mean_moving = window_mean(moving)
    mean_target = window_mean(target)
    var_moving = window_mean(moving * moving) - mean_moving * mean_moving
    var_target = window_mean(target * target) - mean_target * mean_target
    cross_cov = window_mean(moving * target) - mean_moving * mean_target
    moving_core = moving[BOX_R : BOX_R + planes_out]
    target_core = target[BOX_R : BOX_R + planes_out]
    denominator = var_moving * var_target + epsilon
    similarity = cross_cov * cross_cov / denominator
    factor = (
        2.0
        * cross_cov
        / denominator
        * (
            target_core
            - mean_target
            - cross_cov / (var_moving + epsilon) * (moving_core - mean_moving)
        )
    )
    slope_depth = 0.5 * (
        moving[BOX_R + 1 : BOX_R + 1 + planes_out] - moving[BOX_R - 1 : BOX_R - 1 + planes_out]
    )
    padded_rows = jnp.pad(moving_core, ((0, 0), (1, 1), (0, 0)))
    slope_rows = 0.5 * (padded_rows[:, 2:] - padded_rows[:, :-2])
    padded_cols = jnp.pad(moving_core, ((0, 0), (0, 0), (1, 1)))
    slope_cols = 0.5 * (padded_cols[:, :, 2:] - padded_cols[:, :, :-2])
    forces = jnp.stack([factor * slope_depth, factor * slope_rows, factor * slope_cols])
    return (forces, similarity)


def blur_weights():
    bumps = [math.exp(-(offset * offset) / 8.0) for offset in range(-GAUSS_R, GAUSS_R + 1)]
    whole = sum(bumps)
    return [bump / whole for bump in bumps]


def weighted_sum(padded, along, planes_out, weights):
    running = weights[0] * lax.slice_in_dim(padded, 0, planes_out, axis=along)
    for offset in range(1, len(weights)):
        running = running + weights[offset] * lax.slice_in_dim(
            padded, offset, offset + planes_out, axis=along
        )
    return running


def gaussian_blur(padded):
    weights = blur_weights()
    planes_out = padded.shape[1] - 2 * GAUSS_R
    smoothed = weighted_sum(padded, 1, planes_out, weights)
    smoothed = weighted_sum(
        jnp.pad(smoothed, ((0, 0), (0, 0), (GAUSS_R, GAUSS_R), (0, 0))), 2, padded.shape[2], weights
    )
    smoothed = weighted_sum(
        jnp.pad(smoothed, ((0, 0), (0, 0), (0, 0), (GAUSS_R, GAUSS_R))), 3, padded.shape[3], weights
    )
    return smoothed


def on_device(warped):
    moving = warped[0]
    planes = moving.shape[0]
    members = lax.axis_size("subj")
    halo_depth = BOX_R
    template = lax.psum(moving, "subj") / members
    stacked = padded_2(jnp.stack([moving, template]), (("gz", 1),), halo_depth)
    moving_wide = stacked[0]
    target_wide = stacked[1]
    forces, similarity = local_force(moving_wide, target_wide)
    padded = padded_2(forces, (("gz", 1),), GAUSS_R)
    smoothed = gaussian_blur(padded)
    cells = float(lax.axis_size("gz") * planes * moving.shape[1] * moving.shape[2])
    loss = -lax.psum(jnp.sum(similarity), "gz") / cells
    return (smoothed[None], template, jnp.reshape(loss, (1,)))


def solution(mesh):
    placed = (P("subj", "gz", None, None),)
    return jax.shard_map(
        on_device,
        mesh=mesh,
        in_specs=placed,
        out_specs=(P("subj", None, "gz", None, None), P("gz", None, None), P("subj")),
        check_vma=False,
    )
```

profile of v0, /device:TPU:0, one launch (start us, length us, event | category | flops | bytes accessed | tf_op | source)
XLA Modules:
  0.0 339.2 jit_solution(10766948845306653046)
XLA Ops:
  7.2 0.7 all-reduce.16.cloned.1.call-update
  7.9 87.4 %all-reduce.16.cloned.1.call-done = f32[32,64,256]{2,1,0:T(8,128)} async-done(((f32[32,64,256]{2,1,0:T(8,128)}), f32[32,64,256]{2,1,0:T(8,128)}) %all-reduce.16.cloned.1.call-update) | async-done | bytes 2097168 | tf_op jit(solution)/shard_map/psum | solution.py:113
  95.3 1.8 fusion.152
  97.1 0.1 pad_maximum_fusion.4
  97.2 1.3 collective-permute-start
  98.5 1.3 collective-permute-start.1
  99.8 0.2 collective-permute-done
  100.0 5.4 %collective-permute-done.1 = f32[2,4,64,256]{3,2,1,0:T(8,128)S(1)} collective-permute-done((f32[2,4,64,256]{3,2,1,0:T(8,128)S(1)}, f32[2,4,64,256]{3,2,1,0:T(8,128)S(1)}, u32[]{:S(2)}, u32[]{:S(2)}) %collective-permute-start.1) | collective-permute-done | bytes 524320 | tf_op jit(solution)/shard_map/ppermute | solution.py:23
  105.4 0.6 pad_maximum_fusion.2
  106.0 1.4 slice_multiply_fusion.7
  107.4 4.7 %fusion.129 = (f32[32,64,256]{2,1,0:T(8,128)S(1)}, f32[32,64,256]{2,1,0:T(8,128)S(1)}) fusion(f32[1,40,64,256]{3,2,1,0:T(8,128)S(1)} %get-tuple-element.18, f32[1,40,64,256]{3,2,1,0:T(8,128)S(1)} %get-tuple-element.19), kind=kLoop, calls=%fused_computation.241 | loop fusion | flops 8388608 | bytes 41943040 | tf_op jit(solution)/shard_map/add | solution.py:31
  112.1 2.7 fusion.62
  114.9 2.7 fusion.70
  117.6 1.9 fusion.144
  119.5 2.8 fusion.38
  122.3 1.1 pad_maximum_fusion.3
  123.4 7.9 %fusion.137 = (f32[32,64,256]{2,1,0:T(8,128)}, f32[32,64,256]{2,1,0:T(8,128)}) fusion(f32[2,36,64,256]{3,2,1,0:T(8,128)S(1)} %get-tuple-element.22, f32[2,36,64,256]{3,2,1,0:T(8,128)S(1)} %get-tuple-element.23, f32[1,32,64,256]{3,2,1,0:T(8,128)S(1)} %copy-done.2, f32[32,64,256]{2,1,0:T(8,128)} %all-reduce.16.cloned.1.call-done), kind=kLoop, calls=%fused_computation.272 | loop fusion | flops 8912896 | bytes 41943040 | tf_op jit(solution)/shard_map/add | solution.py:31
  131.3 20.2 %fusion.46 = (f32[32,64,256]{2,1,0:T(8,128)}, f32[32,64,256]{2,1,0:T(8,128)}) fusion(f32[32,64,256]{2,1,0:T(8,128)} %get-tuple-element.11, f32[32,64,256]{2,1,0:T(8,128)} %get-tuple-element.12), kind=kLoop, calls=%fused_computation.157 | loop fusion | flops 8388608 | bytes 8388608 | tf_op jit(solution)/shard_map/add | solution.py:31
  151.6 40.5 %fusion.145 = (f32[]{:T(128)}, f32[32,64,256]{2,1,0:T(8,128)}, f32[32,64,256]{2,1,0:T(8,128)}, f32[32,64,256]{2,1,0:T(8,128)}, f32[32,64,256]{2,1,0:T(8,128)}, /*index=5*/f32[32,64,256]{2,1,0:T(8,128)}) fusion(f32[32,64,256]{2,1,0:T(8,128)} %fusion.70, f32[32,64,256]{2,1,0:T(8,128)} %fusion.62, f32[32,64,256]{2,1,0:T(8,128)} %fusion.38, ...), kind=kLoop, calls=%fused_computation.297 | loop fusion | flops 29360128 | bytes 20971524 | tf_op jit(solution)/shard_map/reduce_sum | solution.py:121
  192.1 10.5 %multiply_bitcast_fusion = (f32[1,32,64,256]{3,2,1,0:T(8,128)}, f32[32,64,256]{2,1,0:T(8,128)}) fusion(f32[2,36,64,256]{3,2,1,0:T(8,128)} %copy-done, f32[2,36,64,256]{3,2,1,0:T(8,128)S(1)} %get-tuple-element.22, f32[32,64,256]{2,1,0:T(8,128)} %get-tuple-element.8, f32[1,32,64,256]{3,2,1,0:T(8,128)} %param.1, f32[32,64,256]{2,1,0:T(8,128)} %get-tuple-element.6, ...), kind=kLoop, calls=%fused_computation.295 | loop fusion | flops 6815744 | bytes 23068672 | tf_op jit(solution)/shard_map/stack | solution.py:76
  202.6 2.9 fusion.74
  205.5 0.5 pad_maximum_fusion.1
  206.0 0.9 copy-done.7
  206.9 0.1 fusion.151
  207.0 11.6 %collective-permute-start.2 = (f32[3,3,64,256]{3,2,1,0:T(8,128)S(1)}, f32[3,3,64,256]{3,2,1,0:T(8,128)}, u32[]{:S(2)}, u32[]{:S(2)}) collective-permute-start(f32[3,3,64,256]{3,2,1,0:T(8,128)S(1)} %get-tuple-element.15), channel_id=1, source_target_pairs={{0,1},{1,2},{2,3},{3,4},{4,5},{5,6},{6,7},{7,8},{8,9},{9,10},{10,1... | collective-permute-start | bytes 1769480 | tf_op jit(solution)/shard_map/ppermute | solution.py:22
  218.6 1.3 collective-permute-start.3
  219.9 1.5 broadcast_multiply_fusion
  221.4 38.3 %psum.15 = f32[]{:T(128)} all-reduce(f32[]{:T(128)} %get-tuple-element.3), channel_id=1, replica_groups=mesh['subj'=8,'gz'=16] {'gz'}, use_global_device_ids=true, to_apply=%region_2.3 | all-reduce | flops 1 | bytes 8 | tf_op jit(solution)/shard_map/psum | solution.py:121
  260.3 8.4 %maximum_maximum_fusion = (f32[3,35,64,256]{3,2,1,0:T(8,128)}, f32[3,35,64,256]{3,2,1,0:T(8,128)}) fusion(f32[1,32,64,256]{3,2,1,0:T(8,128)} %copy-done.7, f32[1,32,64,256]{3,2,1,0:T(8,128)S(1)} %get-tuple-element.20, f32[1,32,64,256]{3,2,1,0:T(8,128)} %get-tuple-element.9, f32[3,3,64,256]{3,2,1,0:T(8,128)} %collective-permute-done.2, ...), kind=kLoop, calls=%fused_computation.12 | loop fusion | flops 10321920 | bytes 21233664 | tf_op jit(solution)/shard_map/concatenate | solution.py:24
  268.8 17.9 %fusion.25 = f32[3,32,64,256]{3,2,1,0:T(8,128)} fusion(f32[3,35,64,256]{3,2,1,0:T(8,128)} %get-tuple-element.14, f32[3,35,64,256]{3,2,1,0:T(8,128)} %get-tuple-element.13, f32[1,32,64,256]{3,2,1,0:T(8,128)S(1)} %copy-done.8, f32[1,32,64,256]{3,2,1,0:T(8,128)S(1)} %get-tuple-element.20, f32[1,32,64,256]{3,2,1,0:T(8,128)} %get-tuple-element.9), kind=kLoop, calls=%fused_computation.40 | loop fusion | flops 23592960 | bytes 50331648 | tf_op jit(solution)/shard_map/add | solution.py:89
  286.7 19.3 %fusion.6 = f32[3,32,64,256]{3,2,1,0:T(8,128)} fusion(f32[3,32,64,256]{3,2,1,0:T(8,128)} %fusion.25), kind=kLoop, calls=%fused_computation.20 | loop fusion | flops 20447232 | bytes 12582912 | tf_op jit(solution)/shard_map/add | solution.py:89
  306.0 25.3 %fusion.19 = f32[1,3,32,64,256]{4,3,2,1,0:T(8,128)} fusion(f32[3,32,64,256]{3,2,1,0:T(8,128)} %fusion.6), kind=kLoop, calls=%fused_computation.33 | loop fusion | flops 20447232 | bytes 12582912 | tf_op jit(solution)/shard_map/broadcast_in_dim | solution.py:122
  (22 shorter events, 0.1 us)
Async XLA Ops:
  7.2 88.1 %all-reduce.16.cloned.1.call-start = ((), (), s32[]{:S(2)}) async-start(), calls=%async_computation | async-start | bytes 4194304 | tf_op jit(solution)/shard_map/psum | solution.py:113
  7.9 89.2 %copy-start.1 = (f32[1,32,64,256]{3,2,1,0:T(8,128)S(1)}, f32[1,32,64,256]{3,2,1,0:T(8,128)}, u32[]{:S(2)}) copy-start(f32[1,32,64,256]{3,2,1,0:T(8,128)} %param.1) | copy-start | bytes 6291460
  97.1 8.3 %copy-start.4 = (f32[1,32,64,256]{3,2,1,0:T(8,128)}, f32[1,32,64,256]{3,2,1,0:T(8,128)S(1)}, u32[]{:S(2)}) copy-start(f32[1,32,64,256]{3,2,1,0:T(8,128)S(1)} %fusion.152) | copy-start | bytes 6291460
  97.2 2.8 collective-permute-start
  98.5 6.9 %collective-permute-start.1 = (f32[2,4,64,256]{3,2,1,0:T(8,128)S(1)}, f32[2,4,64,256]{3,2,1,0:T(8,128)S(1)}, u32[]{:S(2)}, u32[]{:S(2)}) collective-permute-start(f32[2,4,64,256]{3,2,1,0:T(8,128)S(1)} %get-tuple-element.24), channel_id=1, source_target_pairs={{1,0},{2,1},{3,2},{4,3},{5,4},{6,5},{7,6},{8,7},{9,8},{10,9},{11,1... | collective-permute-start | bytes 1572872 | tf_op jit(solution)/shard_map/ppermute | solution.py:23
  119.5 2.8 copy-start.2
  119.5 2.8 copy-start.5
  123.4 7.9 %copy-start = (f32[2,36,64,256]{3,2,1,0:T(8,128)}, f32[2,36,64,256]{3,2,1,0:T(8,128)S(1)}, u32[]{:S(2)}) copy-start(f32[2,36,64,256]{3,2,1,0:T(8,128)S(1)} %get-tuple-element.23) | copy-start | bytes 14155780
  192.1 10.5 %copy-start.3 = (f32[1,32,64,256]{3,2,1,0:T(8,128)S(1)}, f32[1,32,64,256]{3,2,1,0:T(8,128)}, u32[]{:S(2)}) copy-start(f32[1,32,64,256]{3,2,1,0:T(8,128)} %param.1) | copy-start | bytes 6291460
  202.6 2.9 copy-start.9
  205.5 1.4 copy-start.7
  206.9 13.0 %copy-start.6 = (f32[32,64,256]{2,1,0:T(8,128)S(1)}, f32[32,64,256]{2,1,0:T(8,128)}, u32[]{:S(2)}) copy-start(f32[32,64,256]{2,1,0:T(8,128)} %all-reduce.16.cloned.1.call-done) | copy-start | bytes 6291460
  207.0 53.3 %collective-permute-start.2 = (f32[3,3,64,256]{3,2,1,0:T(8,128)S(1)}, f32[3,3,64,256]{3,2,1,0:T(8,128)}, u32[]{:S(2)}, u32[]{:S(2)}) collective-permute-start(f32[3,3,64,256]{3,2,1,0:T(8,128)S(1)} %get-tuple-element.15), channel_id=1, source_target_pairs={{0,1},{1,2},{2,3},{3,4},{4,5},{5,6},{6,7},{7,8},{8,9},{9,10},{10,1... | collective-permute-start | bytes 1769480 | tf_op jit(solution)/shard_map/ppermute | solution.py:22
  218.6 41.7 %collective-permute-start.3 = (f32[3,3,64,256]{3,2,1,0:T(8,128)S(1)}, f32[3,3,64,256]{3,2,1,0:T(8,128)}, u32[]{:S(2)}, u32[]{:S(2)}) collective-permute-start(f32[3,3,64,256]{3,2,1,0:T(8,128)S(1)} %get-tuple-element.16), channel_id=1, source_target_pairs={{1,0},{2,1},{3,2},{4,3},{5,4},{6,5},{7,6},{8,7},{9,8},{10,9},{11,1... | collective-permute-start | bytes 1769480 | tf_op jit(solution)/shard_map/ppermute | solution.py:23
  260.3 8.5 %copy-start.8 = (f32[1,32,64,256]{3,2,1,0:T(8,128)S(1)}, f32[1,32,64,256]{3,2,1,0:T(8,128)}, u32[]{:S(2)}) copy-start(f32[1,32,64,256]{3,2,1,0:T(8,128)} %copy-done.7) | copy-start | bytes 6291460
Sparse Core Ops, SparseCore 0:
  10.5 84.7 all-reduce.15
where the time goes:
time: 340 us; the launch traced here: 339 us
  other arithmetic  175 us (51%)
  waiting for transfers between devices  93.6 us (28%)
  blocking collectives  38.3 us (11%)
  between operations  16 us (5%)
  starting transfers between devices  15.5 us (5%)
    psum x1, waiting for transfers between devices, on_device(): template = lax.psum(moving, 'subj') / members  87.4 us
    add x7, other arithmetic, shifted_sum(): running + lax.slice_in_dim(padded, offset, offset + planes_out, axis=along)  42.9 us
    reduce_sum x1, other arithmetic, on_device(): loss = -lax.psum(jnp.sum(similarity), 'gz') / cells  40.5 us
    psum x1, blocking collectives, on_device(): loss = -lax.psum(jnp.sum(similarity), 'gz') / cells  38.3 us
    add x2, other arithmetic, weighted_sum(): running + weights[offset] * lax.slice_in_dim(padded, offset, offset + pla...  37.2 us
    broadcast_in_dim x1, other arithmetic, on_device(): return (smoothed[None], template, jnp.reshape(loss, (1,)))  25.3 us
    another operation x3, other arithmetic, local_force(): jnp.stack([factor * slope_depth, factor * slope_rows, factor * slope_cols])  13.9 us
    ppermute x2, starting transfers between devices, padded_2(): before = lax.ppermute(last, axis, up)  12.9 us
  transfers between devices with their start and end apart: 5, of which 3 were waited for; matrix products, arithmetic and copies ran while one was open for 0% of the time, Pallas kernels for 0%

commit v1 on v0

v1 whole, which is shorter than its diff:
```python
import functools, math
import numpy as np
import jax
import jax.numpy as jnp
from jax import lax
from jax.experimental import pallas as pl
from jax.experimental.pallas import tpu as pltpu

BOX_R = 4
GAUSS_R = 3
epsilon = 1e-05
F32, BF16 = jnp.float32, jnp.bfloat16
H = 7
BZ = 8
INV = 1.0 / 729.0


def blur_weights():
    bumps = [math.exp(-(k * k) / 8.0) for k in range(-GAUSS_R, GAUSS_R + 1)]
    whole = sum(bumps)
    return [b / whole for b in bumps]


def band_ones(nx):
    d = np.abs(np.arange(nx)[:, None] - np.arange(nx)[None, :])
    b = (d <= BOX_R).astype(np.float32)
    return np.concatenate([b, b, b], axis=0)


def split2(m):
    hi = m.astype(jnp.bfloat16).astype(np.float32)
    lo = (m - hi).astype(np.float32)
    return hi, lo


def gauss_x(nx):
    w = np.array(blur_weights(), np.float32)
    d = np.arange(nx)[:, None] - np.arange(nx)[None, :]
    m = np.where(np.abs(d) <= GAUSS_R, w[np.clip(d + GAUSS_R, 0, 2 * GAUSS_R)], 0.0).astype(np.float32)
    hi, lo = split2(m)
    return np.concatenate([hi, hi, lo], axis=0)


def row_of(ny):
    nb = ny // 8
    r = np.arange(ny)
    i, s = r // 8, r % 8
    return s * nb + i


def gauss_y(ny, planes):
    w = np.array(blur_weights(), np.float32)
    y_in = row_of(ny)
    d = y_in[None, :] - np.arange(ny)[:, None]
    m = np.where(np.abs(d) <= GAUSS_R, w[np.clip(d + GAUSS_R, 0, 2 * GAUSS_R)], 0.0).astype(np.float32)
    m = np.kron(np.eye(planes, dtype=np.float32), m)
    hi, lo = split2(m)
    return np.concatenate([hi, hi, lo], axis=1)


def suffix_prefix(first, second):
    n = len(first)
    suf = [None] * n
    suf[n - 1] = first[n - 1]
    for i in range(n - 2, -1, -1):
        suf[i] = first[i] + suf[i + 1]
    out = []
    run = None
    for i in range(n):
        run = second[i] if run is None else run + second[i]
        out.append(suf[i] + run)
    return out


def permute_in(dst, dst_plane, src, src_plane, n, stage):
    def natural(p, c):
        for h in range(2):
            stage[p, h] = src[src_plane + p, :, pl.ds(128 * h, 128)]
        return c
    lax.fori_loop(0, n, natural, 0)

    def body(p, c):
        for i in range(8):
            for h in range(2):
                dst[dst_plane + p, pl.ds(8 * i, 8), pl.ds(128 * h, 128)] = stage[
                    p, h, pl.ds(i, 8, stride=8), :]
        return c
    lax.fori_loop(0, n, body, 0)


def z_sums(out, terms, get_first, get_second):
    def body(q, c):
        rows = pl.ds(pl.multiple_of(q * 8, 8), 8)
        for h in range(2):
            cols = pl.ds(128 * h, 128)
            first = get_first(rows, cols)
            second = get_second(rows, cols)
            for ref, term in zip(out, terms):
                res = suffix_prefix([term(a) for a in first], [term(b) for b in second])
                for p in range(8):
                    ref[p, rows, cols] = res[p]
        return c
    lax.fori_loop(0, 8, body, 0)


def y_sums_split(ref, parts):
    sub = lax.broadcasted_iota(jnp.int32, (8, 128), 0)
    first_row, last_row = sub == 0, sub == 7

    def body(p, c):
        for h in range(2):
            cols = pl.ds(128 * h, 128)
            x = [ref[p, pl.ds(8 * i, 8), cols] for i in range(8)]
            down = [jnp.where(first_row, 0.0, pltpu.roll(x[i], 1, 0)) for i in range(4, 8)]
            up = [jnp.where(last_row, 0.0, pltpu.roll(x[i], 7, 0)) for i in range(4)]
            res = suffix_prefix(down + x[:4], x[4:] + up)
            for j in range(4):
                v = jnp.concatenate([res[2 * j], res[2 * j + 1]], axis=0)
                hi = v.astype(BF16)
                v = v - hi.astype(F32)
                mid = v.astype(BF16)
                lo = (v - mid.astype(F32)).astype(BF16)
                rows = pl.ds(pl.multiple_of(p * 64, 64) + 16 * j, 16)
                parts[rows, pl.ds(128 * h, 128)] = hi
                parts[rows, pl.ds(256 + 128 * h, 128)] = mid
                parts[rows, pl.ds(512 + 128 * h, 128)] = lo
        return c
    lax.fori_loop(0, 8, body, 0)


def x_sums(parts, band, out):
    out[...] = jnp.dot(parts[...], band[...], preferred_element_type=F32).reshape(out.shape)


def fetch_block(k, last, ring, slot, lo, body, hi, stage):
    @pl.when(k == 0)
    def _():
        ring[slot, 0] = jnp.zeros(ring.shape[2:], F32)
        permute_in(ring.at[slot], 1, lo, 0, H, stage)

    @pl.when(jnp.logical_and(k > 0, k < last))
    def _():
        permute_in(ring.at[slot], 0, body, 0, BZ, stage)

    @pl.when(k == last)
    def _():
        permute_in(ring.at[slot], 0, hi, 0, H, stage)
        ring[slot, 7] = jnp.zeros(ring.shape[2:], F32)


def moving_kernel(lo, body, hi, band, ip, mean, var, ring, zs, parts, sums, stage):
    k = pl.program_id(0)
    last = pl.num_programs(0) - 1
    slot = lax.rem(k, 2)
    prev = 1 - slot
    fetch_block(k, last, ring, slot, lo, body, hi, stage)
    ip[...] = ring[slot]

    @pl.when(k > 0)
    def _():
        z_sums(
            [zs.at[0], zs.at[1]],
            [lambda a: a, lambda a: a * a],
            lambda r, c: [ring[prev, p, r, c] for p in range(8)],
            lambda r, c: [ring[slot, p, r, c] for p in range(8)],
        )
        for v in range(2):
            y_sums_split(zs.at[v], parts)
            x_sums(parts, band, sums.at[v])

        def point(p, c):
            m = sums[0, p] * INV
            mean[p] = m
            var[p] = sums[1, p] * INV - m * m
            return c
        lax.fori_loop(0, 8, point, 0)


def blk(f):
    return pl.BlockSpec((BZ, 64, 256), f)


def whole(shape):
    return pl.BlockSpec(shape, lambda k: (0,) * len(shape))


def params(**kw):
    return pltpu.CompilerParams(vmem_limit_bytes=60 * 1024 * 1024, **kw)


def moving_call(moving, lo, hi):
    n = moving.shape[0] // BZ
    plane = moving.shape[1:]
    band = jnp.asarray(band_ones(256), BF16)
    clip = lambda k: jnp.clip(k - 1, 0, n - 1)
    return pl.pallas_call(
        moving_kernel,
        name="moving",
        grid=(n + 2,),
        in_specs=[whole(lo.shape), blk(lambda k: (clip(k), 0, 0)), whole(hi.shape), whole(band.shape)],
        out_specs=[blk(lambda k: (k, 0, 0)), blk(lambda k: (jnp.maximum(k - 1, 0), 0, 0)), blk(lambda k: (jnp.maximum(k - 1, 0), 0, 0))],
        out_shape=[jax.ShapeDtypeStruct(((n + 2) * BZ,) + plane, F32)] + [jax.ShapeDtypeStruct(((n + 1) * BZ,) + plane, F32)] * 2,
        scratch_shapes=[
            pltpu.VMEM((2, BZ, 64, 256), F32),
            pltpu.VMEM((2, BZ, 64, 256), F32),
            pltpu.VMEM((BZ * 64, 768), BF16),
            pltpu.VMEM((2, BZ, 64, 256), F32),
            pltpu.VMEM((BZ, 2, 64, 128), F32),
        ],
        compiler_params=params(),
    )(lo, moving, hi, band)


def factor_kernel(edge, lo, body, hi, ia, ib, mean, var, band, fac, loss, ring, zs, parts, sums, stage):
    k = pl.program_id(0)
    last = pl.num_programs(0) - 1
    slot = lax.rem(k, 2)
    prev = 1 - slot
    fetch_block(k, last, ring, slot, lo, body, hi, stage)

    @pl.when(k == 0)
    def _():
        loss[...] = jnp.zeros(loss.shape, F32)

    @pl.when(k > 0)
    def _():
        z_sums(
            [zs.at[0], zs.at[1]],
            [lambda a: a, lambda a: a * a],
            lambda r, c: [ring[prev, p, r, c] for p in range(8)],
            lambda r, c: [ring[slot, p, r, c] for p in range(8)],
        )
        z_sums(
            [zs.at[2]],
            [lambda a: a[0] * a[1]],
            lambda r, c: [(ring[prev, p, r, c], ia[p, r, c]) for p in range(8)],
            lambda r, c: [(ring[slot, p, r, c], ib[p, r, c]) for p in range(8)],
        )
        for v in range(3):
            y_sums_split(zs.at[v], parts)
            x_sums(parts, band, sums.at[v])

        def point(t, c):
            p = t >> 2
            rows = pl.ds(pl.multiple_of(lax.rem(t, 4) * 16, 16), 16)
            plane = (k - 1) * BZ - 4 + p
            inside = jnp.logical_and(plane >= 0, plane < (last - 1) * BZ)
            keep = jnp.logical_or(inside, jnp.where(plane < 0, edge[0], edge[1]) == 0)
            src_slot = jnp.where(p < 4, prev, slot)
            q = jnp.where(p < 4, p + 4, p - 4)
            j0 = ring[src_slot, q, rows, :]
            i0 = jnp.where(p < 4, ia[q, rows, :], ib[q, rows, :])
            mj = sums[0, p, rows, :] * INV
            vj = sums[1, p, rows, :] * INV - mj * mj
            mi = mean[p, rows, :]
            vi = var[p, rows, :]
            cc = sums[2, p, rows, :] * INV - mi * mj
            d1 = vi * vj + epsilon
            e = cc / d1
            sim = cc * e
            f = e * ((j0 - mj) - cc / (vi + epsilon) * (i0 - mi))
            fac[p, rows, :] = jnp.where(keep, f, 0.0)
            loss[...] += jnp.where(inside, sim, 0.0)
            return c
        lax.fori_loop(0, 32, point, 0)


def factor_call(edge, template, lo, hi, ip, mean, var):
    n = template.shape[0] // BZ
    plane = template.shape[1:]
    band = jnp.asarray(band_ones(256), BF16)
    clip = lambda k: jnp.clip(k - 1, 0, n - 1)
    back = lambda k: jnp.maximum(k - 1, 0)
    return pl.pallas_call(
        factor_kernel,
        name="factor",
        grid=(n + 2,),
        in_specs=[
            pl.BlockSpec(memory_space=pltpu.SMEM),
            whole(lo.shape), blk(lambda k: (clip(k), 0, 0)), whole(hi.shape),
            blk(lambda k: (back(k), 0, 0)), blk(lambda k: (jnp.maximum(k, 1), 0, 0)),
            blk(lambda k: (back(k), 0, 0)), blk(lambda k: (back(k), 0, 0)),
            whole(band.shape),
        ],
        out_specs=[blk(lambda k: (back(k), 0, 0)), whole((16, 256))],
        out_shape=[jax.ShapeDtypeStruct(((n + 1) * BZ,) + plane, F32), jax.ShapeDtypeStruct((16, 256), F32)],
        scratch_shapes=[
            pltpu.VMEM((2, BZ, 64, 256), F32),
            pltpu.VMEM((3, BZ, 64, 256), F32),
            pltpu.VMEM((BZ * 64, 768), BF16),
            pltpu.VMEM((3, BZ, 64, 256), F32),
            pltpu.VMEM((BZ, 2, 64, 128), F32),
        ],
        compiler_params=params(),
    )(edge, lo, template, hi, ip, ip, mean, var, band)


def smooth_kernel(fac, ia, ib, ax, ay, out, ring, xp, xs, yp):
    k = pl.program_id(0)
    slot = lax.rem(k, 2)
    prev = 1 - slot
    sub = lax.broadcasted_iota(jnp.int32, (8, 128), 0)
    lane = lax.broadcasted_iota(jnp.int32, (8, 128), 1)

    def raw(p, q, mid, before, after):
        f = [[fac[p, pl.ds(8 * i, 8), pl.ds(128 * h, 128)] for h in range(2)] for i in range(8)]
        im = [[mid[q, pl.ds(8 * i, 8), pl.ds(128 * h, 128)] for h in range(2)] for i in range(8)]
        for i in range(8):
            rows = pl.ds(8 * i, 8)
            for h in range(2):
                cols = pl.ds(128 * h, 128)
                ring[slot, 0, p, rows, cols] = f[i][h] * (after(rows, cols) - before(rows, cols))
                up = im[i + 1][h] if i < 7 else jnp.where(sub == 7, 0.0, pltpu.roll(im[0][h], 7, 0))
                dn = im[i - 1][h] if i > 0 else jnp.where(sub == 0, 0.0, pltpu.roll(im[7][h], 1, 0))
                ring[slot, 1, p, rows, cols] = f[i][h] * (up - dn)
            left = [pltpu.roll(im[i][h], 127, 1) for h in range(2)]
            right = [pltpu.roll(im[i][h], 1, 1) for h in range(2)]
            e, s = lane == 127, lane == 0
            nxt = [jnp.where(e, left[1], left[0]), jnp.where(e, 0.0, left[1])]
            prv = [jnp.where(s, 0.0, right[0]), jnp.where(s, right[0], right[1])]
            for h in range(2):
                ring[slot, 2, p, rows, pl.ds(128 * h, 128)] = f[i][h] * (nxt[h] - prv[h])

    def lower(p, c):
        raw(p, p + 4, ia, lambda r, cc: ia[p + 3, r, cc], lambda r, cc: ia[p + 5, r, cc])
        return c

    def upper(p, c):
        raw(p, p - 4, ib, lambda r, cc: ib[p - 5, r, cc], lambda r, cc: ib[p - 3, r, cc])
        return c
    lax.fori_loop(0, 3, lower, 0)
    raw(3, 7, ia, lambda r, cc: ia[6, r, cc], lambda r, cc: ib[0, r, cc])
    raw(4, 0, ib, lambda r, cc: ia[7, r, cc], lambda r, cc: ib[1, r, cc])
    lax.fori_loop(5, 8, upper, 0)

    w = [float(v) for v in blur_weights()]

    @pl.when(k > 0)
    def _():
        for comp in range(3):
            def z_pass(q, c):
                rows = pl.ds(pl.multiple_of(q * 16, 16), 16)
                for h in range(2):
                    cols = pl.ds(128 * h, 128)
                    x = [ring[prev, comp, p, rows, cols] for p in range(1, 8)] + [
                        ring[slot, comp, p, rows, cols] for p in range(0, 7)]
                    for p in range(8):
                        v = w[3] * x[p + 3]
                        for d in range(1, 4):
                            v = v + w[3 - d] * (x[p + 3 - d] + x[p + 3 + d])
                        hi = v.astype(BF16)
                        lo = (v - hi.astype(F32)).astype(BF16)
                        dst = pl.ds(64 * p + pl.multiple_of(q * 16, 16), 16)
                        xp[dst, pl.ds(128 * h, 128)] = hi
                        xp[dst, pl.ds(256 + 128 * h, 128)] = lo
                        xp[dst, pl.ds(512 + 128 * h, 128)] = hi
                return c
            lax.fori_loop(0, 4, z_pass, 0)
            xs[...] = jnp.dot(xp[...], ax[...], preferred_element_type=F32)

            def split(t, c):
                rows = pl.ds(pl.multiple_of(t * 32, 32), 32)
                v = xs[rows, :]
                hi = v.astype(BF16)
                g = t >> 3
                r = pl.multiple_of(lax.rem(t, 8) * 32, 32)
                yp[g, pl.ds(r, 32), :] = hi
                yp[g, pl.ds(256 + r, 32), :] = (v - hi.astype(F32)).astype(BF16)
                yp[g, pl.ds(512 + r, 32), :] = hi
                return c
            lax.fori_loop(0, 16, split, 0)
            for g in range(2):
                out[comp, pl.ds(4 * g, 4)] = jnp.dot(
                    ay[...], yp[g], preferred_element_type=F32).reshape(4, 64, 256)


def smooth_call(fac, ip):
    n = fac.shape[0] // BZ - 1
    plane = fac.shape[1:]
    ax = jnp.asarray(gauss_x(256), BF16)
    ay = jnp.asarray(gauss_y(64, 4), BF16)
    return pl.pallas_call(
        smooth_kernel,
        name="smooth",
        grid=(n + 1,),
        in_specs=[blk(lambda k: (k, 0, 0)), blk(lambda k: (k, 0, 0)), blk(lambda k: (k + 1, 0, 0)),
                  whole(ax.shape), whole(ay.shape)],
        out_specs=pl.BlockSpec((3, BZ, 64, 256), lambda k: (0, jnp.maximum(k - 1, 0), 0, 0)),
        out_shape=jax.ShapeDtypeStruct((3, n * BZ) + plane, F32),
        scratch_shapes=[
            pltpu.VMEM((2, 3, BZ, 64, 256), F32),
            pltpu.VMEM((BZ * 64, 768), BF16),
            pltpu.VMEM((BZ * 64, 256), F32),
            pltpu.VMEM((2, 768, 256), BF16),
        ],
        compiler_params=params(),
    )(fac, ip, ip, ax, ay)


from jax.sharding import PartitionSpec as P


def halos(array, axis, width):
    size = lax.axis_size(axis)
    up = [(i, i + 1) for i in range(size - 1)]
    down = [(j, i) for i, j in up]
    lo = lax.ppermute(array[-width:], axis, up)
    hi = lax.ppermute(array[:width], axis, down)
    return lo, hi


def on_device(warped):
    moving = warped[0]
    planes = moving.shape[0]
    g, size = lax.axis_index("gz"), lax.axis_size("gz")
    edge = jnp.stack([g == 0, g == size - 1]).astype(jnp.int32)
    lo, hi = halos(moving, "gz", H)
    template = lax.psum(moving, "subj") / lax.axis_size("subj")
    ip, mean, var = moving_call(moving, lo, hi)
    tlo, thi = halos(template, "gz", H)
    fac, part = factor_call(edge, template, tlo, thi, ip, mean, var)
    cells = float(size * planes * moving.shape[1] * moving.shape[2])
    loss = -lax.psum(jnp.sum(part), "gz") / cells
    force = smooth_call(fac, ip)
    return force[None], template, jnp.reshape(loss, (1,))


def solution(mesh):
    return jax.shard_map(
        on_device,
        mesh=mesh,
        in_specs=(P("subj", "gz", None, None),),
        out_specs=(P("subj", None, "gz", None, None), P("gz", None, None), P("subj")),
        check_vma=False,
    )
```

time: 340 us -> 241 us (0.71)
  other arithmetic: 175 us -> 3.73 us
  Pallas kernels: 0 us -> 64.3 us
  waiting for transfers between devices: 93.6 us -> 101 us
  starting transfers between devices: 15.5 us -> 9.5 us
  blocking collectives: 38.3 us -> 43.3 us
    add x9 -> x0, other arithmetic: 80.1 us -> none  [the longest x7 42.9 us: shifted_sum(): running + lax.slice_in_dim(padded, offset, offset + planes_out, axis=along)]
    pallas_call x0 -> x3, Pallas kernels: none -> 64.3 us  [the longest x1 26.3 us: smooth_call(): pl.pallas_call(smooth_kernel, name='smooth', grid=(n + 1,), in_specs=[blk...]
    reduce_sum x1, other arithmetic: 40.5 us -> 1.32 us  [on_device(): loss = -lax.psum(jnp.sum(part), 'gz') / cells]
    broadcast_in_dim x1 -> x0, other arithmetic: 25.3 us -> none  [on_device(): return (smoothed[None], template, jnp.reshape(loss, (1,)))]
    another operation x5 -> x0, other arithmetic: 15.8 us -> none  [the longest x3 13.9 us: local_force(): jnp.stack([factor * slope_depth, factor * slope_rows, factor * slope_cols])]
    psum x1, waiting for transfers between devices: 87.4 us -> 98.8 us  [on_device(): template = lax.psum(moving, 'subj') / lax.axis_size('subj')]
    concatenate x3 -> x0, other arithmetic: 10.2 us -> none  [padded_2(): array = jnp.concatenate([before, array, after], axis=dim)]
    ppermute x4, starting transfers between devices: 15.5 us -> 9.5 us  [the longest x2 6.91 us: halos(): lo = lax.ppermute(array[-width:], axis, up)]
where the time goes in v1:
time: 241 us; the launch traced here: 240 us
  waiting for transfers between devices  101 us (42%)
  Pallas kernels  64.3 us (27%)
  blocking collectives  43.3 us (18%)
  between operations  15.9 us (7%)
  starting transfers between devices  9.5 us (4%)
  other arithmetic  3.73 us (2%)
  local copies, waits for them, and re-layouts  2.79 us (1%)
    psum x1, waiting for transfers between devices, on_device(): template = lax.psum(moving, 'subj') / lax.axis_size('subj')  98.8 us
    psum x1, blocking collectives, on_device(): loss = -lax.psum(jnp.sum(part), 'gz') / cells  43.3 us
    pallas_call x1, Pallas kernels, smooth_call(): pl.pallas_call(smooth_kernel, name='smooth', grid=(n + 1,), in_specs=[blk...  26.3 us
    pallas_call x1, Pallas kernels, factor_call(): pl.pallas_call(factor_kernel, name='factor', grid=(n + 2,), in_specs=[pl....  23.5 us
    pallas_call x1, Pallas kernels, moving_call(): pl.pallas_call(moving_kernel, name='moving', grid=(n + 2,), in_specs=[who...  14.5 us
    ppermute x2, starting transfers between devices, halos(): lo = lax.ppermute(array[-width:], axis, up)  6.91 us
  transfers between devices with their start and end apart: 5, of which 3 were waited for; matrix products, arithmetic and copies ran while one was open for 0% of the time, Pallas kernels for 0%

profile of v1, /device:TPU:0, one launch (start us, length us, event | category | flops | bytes accessed | tf_op | source)
XLA Modules:
  0.0 240.4 jit_solution(11877424200893438702)
XLA Ops:
  7.2 1.2 slice_bitcast_fusion
  8.4 1.3 collective-permute-start.3
  9.7 3.1 %collective-permute-start.2 = (f32[7,64,256]{2,1,0:T(8,128)S(1)}, f32[7,64,256]{2,1,0:T(8,128)S(1)}, u32[]{:S(2)}, u32[]{:S(2)}) collective-permute-start(f32[7,64,256]{2,1,0:T(8,128)S(1)} %get-tuple-element.14), channel_id=1, source_target_pairs={{0,1},{1,2},{2,3},{3,4},{4,5},{5,6},{6,7},{7,8},{8,9},{9,10},{10,1... | collective-permute-start | bytes 1376264 | tf_op jit(solution)/shard_map/ppermute | solution.py:407
  12.8 0.0 collective-permute-done.3.hi
  12.8 0.0 copy-start.2
  12.8 1.4 collective-permute-done.2.lo
  14.2 0.0 copy-start.3
  14.2 0.0 copy-done.2
  14.2 0.8 copy-done.3
  14.9 14.5 %moving.1 = (f32[48,64,256]{2,1,0:T(8,128)}, f32[40,64,256]{2,1,0:T(8,128)}, f32[40,64,256]{2,1,0:T(8,128)}) custom-call(f32[7,64,256]{2,1,0:T(8,128)} %copy-done.3, f32[32,64,256]{2,1,0:T(8,128)} %bitcast.9, f32[7,64,256]{2,1,0:T(8,128)} %copy-done.2, bf16[768,256]{1,0:T(8,128)(2,1)} %constant.22.clone.band), custom_call_target="tpu_custom_call" | custom-call | tf_op jit(solution)/shard_map/moving/pallas_call | solution.py:196
  29.4 0.0 all-reduce.2.cloned.1.call-start
  29.4 0.7 all-reduce.2.cloned.1.call-update
  30.1 98.8 %all-reduce.2.cloned.1.call-done = f32[32,64,256]{2,1,0:T(8,128)} async-done(((f32[32,64,256]{2,1,0:T(8,128)}), f32[32,64,256]{2,1,0:T(8,128)}) %all-reduce.2.cloned.1.call-update) | async-done | bytes 2097168 | tf_op jit(solution)/shard_map/psum | solution.py:418
  128.9 1.8 broadcast_multiply_fusion.body
  130.7 0.0 copy-start
  130.7 0.1 fusion
  130.8 1.3 collective-permute-start.1
  132.1 3.9 %collective-permute-start = (f32[7,64,256]{2,1,0:T(8,128)S(1)}, f32[7,64,256]{2,1,0:T(8,128)}, u32[]{:S(2)}, u32[]{:S(2)}) collective-permute-start(f32[7,64,256]{2,1,0:T(8,128)S(1)} %get-tuple-element.16), channel_id=1, source_target_pairs={{0,1},{1,2},{2,3},{3,4},{4,5},{5,6},{6,7},{7,8},{8,9},{9,10},{10,1... | collective-permute-start | bytes 1376264 | tf_op jit(solution)/shard_map/ppermute | solution.py:407
  135.9 0.6 add_convert_fusion.edge
  136.5 0.0 collective-permute-done.1.hi
  136.5 0.0 copy-start.1
  136.6 0.1 collective-permute-done.lo
  136.6 0.0 copy-done
  136.7 0.7 copy-done.1
  137.4 23.5 %factor.1 = (f32[40,64,256]{2,1,0:T(8,128)}, f32[16,256]{1,0:T(8,128)}) custom-call(s32[2]{0:T(128)} %add_convert_fusion.edge, f32[7,64,256]{2,1,0:T(8,128)} %collective-permute-done.lo, f32[32,64,256]{2,1,0:T(8,128)} %copy-done, f32[7,64,256]{2,1,0:T(8,128)} %copy-done.1, f32[48,64,256]{2,1,0:T(8,128)} %get-tuple-element.8.ia.ib, ...), custom_call_target="tpu_custom_call" | custom-call | tf_op jit(solution)/shard_map/factor/pallas_call | solution.py:274
  160.9 1.3 reduce_sum.9
  162.2 43.3 %psum.15 = f32[]{:T(128)} all-reduce(f32[]{:T(128)} %reduce_sum.9), channel_id=1, replica_groups=mesh['subj'=8,'gz'=16] {'gz'}, use_global_device_ids=true, to_apply=%region_2.0 | all-reduce | flops 1 | bytes 8 | tf_op jit(solution)/shard_map/psum | solution.py:423
  206.1 26.3 %smooth.1 = f32[3,32,64,256]{3,2,1,0:T(8,128)} custom-call(f32[40,64,256]{2,1,0:T(8,128)} %get-tuple-element.11.fac, f32[48,64,256]{2,1,0:T(8,128)} %get-tuple-element.8.ia.ib, f32[48,64,256]{2,1,0:T(8,128)} %get-tuple-element.8.ia.ib, bf16[768,256]{1,0:T(8,128)(2,1)} %constant.23.clone.ax, bf16[256,768]{1,0:T(8,128)(2,1)} %constant.24.clone.ay), custom_call_target="tpu_custom_call" | custom-call | tf_op jit(solution)/shard_map/smooth/pallas_call | solution.py:382
Async XLA Ops:
  8.4 4.4 %collective-permute-start.3 = (f32[7,64,256]{2,1,0:T(8,128)S(1)}, f32[7,64,256]{2,1,0:T(8,128)S(1)}, u32[]{:S(2)}, u32[]{:S(2)}) collective-permute-start(f32[7,64,256]{2,1,0:T(8,128)S(1)} %get-tuple-element.13), channel_id=1, source_target_pairs={{1,0},{2,1},{3,2},{4,3},{5,4},{6,5},{7,6},{8,7},{9,8},{10,9},{11,1... | collective-permute-start | bytes 1376264 | tf_op jit(solution)/shard_map/ppermute | solution.py:408
  9.7 4.5 %collective-permute-start.2 = (f32[7,64,256]{2,1,0:T(8,128)S(1)}, f32[7,64,256]{2,1,0:T(8,128)S(1)}, u32[]{:S(2)}, u32[]{:S(2)}) collective-permute-start(f32[7,64,256]{2,1,0:T(8,128)S(1)} %get-tuple-element.14), channel_id=1, source_target_pairs={{0,1},{1,2},{2,3},{3,4},{4,5},{5,6},{6,7},{7,8},{8,9},{9,10},{10,1... | collective-permute-start | bytes 1376264 | tf_op jit(solution)/shard_map/ppermute | solution.py:407
  12.8 1.4 copy-start.2
  14.2 0.8 copy-start.3
  29.4 99.5 %all-reduce.2.cloned.1.call-start = ((), (), s32[]{:S(2)}) async-start(), calls=%async_computation | async-start | bytes 4194304 | tf_op jit(solution)/shard_map/psum | solution.py:418
  130.7 6.0 %copy-start = (f32[32,64,256]{2,1,0:T(8,128)}, f32[32,64,256]{2,1,0:T(8,128)S(1)}, u32[]{:S(2)}) copy-start(f32[32,64,256]{2,1,0:T(8,128)S(1)} %broadcast_multiply_fusion.body) | copy-start | bytes 6291460
  130.8 5.8 %collective-permute-start.1 = (f32[7,64,256]{2,1,0:T(8,128)S(1)}, f32[7,64,256]{2,1,0:T(8,128)S(1)}, u32[]{:S(2)}, u32[]{:S(2)}) collective-permute-start(f32[7,64,256]{2,1,0:T(8,128)S(1)} %get-tuple-element.15), channel_id=1, source_target_pairs={{1,0},{2,1},{3,2},{4,3},{5,4},{6,5},{7,6},{8,7},{9,8},{10,9},{11,1... | collective-permute-start | bytes 1376264 | tf_op jit(solution)/shard_map/ppermute | solution.py:408
  132.1 4.6 %collective-permute-start = (f32[7,64,256]{2,1,0:T(8,128)S(1)}, f32[7,64,256]{2,1,0:T(8,128)}, u32[]{:S(2)}, u32[]{:S(2)}) collective-permute-start(f32[7,64,256]{2,1,0:T(8,128)S(1)} %get-tuple-element.16), channel_id=1, source_target_pairs={{0,1},{1,2},{2,3},{3,4},{4,5},{5,6},{6,7},{7,8},{8,9},{9,10},{10,1... | collective-permute-start | bytes 1376264 | tf_op jit(solution)/shard_map/ppermute | solution.py:407
  136.5 0.8 copy-start.1
Sparse Core Ops, SparseCore 0:
  32.7 96.1 all-reduce.1

commit v2 on v0

v2 whole, which is shorter than its diff:
```python
import functools, math
import numpy as np
import jax
import jax.numpy as jnp
from jax import lax
from jax.experimental import pallas as pl
from jax.experimental.pallas import tpu as pltpu

BOX_R = 4
GAUSS_R = 3
epsilon = 1e-05
F32, BF16 = jnp.float32, jnp.bfloat16
BZ = 8
INV = 1.0 / 729.0


def blur_weights():
    bumps = [math.exp(-(k * k) / 8.0) for k in range(-GAUSS_R, GAUSS_R + 1)]
    whole = sum(bumps)
    return [b / whole for b in bumps]


def band_ones(nx):
    d = np.abs(np.arange(nx)[:, None] - np.arange(nx)[None, :])
    b = (d <= BOX_R).astype(np.float32)
    return np.concatenate([b, b, b], axis=0)


def split2(m):
    hi = m.astype(jnp.bfloat16).astype(np.float32)
    lo = (m - hi).astype(np.float32)
    return hi, lo


def gauss_x(nx):
    w = np.array(blur_weights(), np.float32)
    d = np.arange(nx)[:, None] - np.arange(nx)[None, :]
    m = np.where(np.abs(d) <= GAUSS_R, w[np.clip(d + GAUSS_R, 0, 2 * GAUSS_R)], 0.0).astype(np.float32)
    hi, lo = split2(m)
    return np.concatenate([hi, hi, lo], axis=0)


def row_of(ny):
    nb = ny // 8
    r = np.arange(ny)
    i, s = r // 8, r % 8
    return s * nb + i


def gauss_y(ny, planes):
    w = np.array(blur_weights(), np.float32)
    y_in = row_of(ny)
    d = y_in[None, :] - np.arange(ny)[:, None]
    m = np.where(np.abs(d) <= GAUSS_R, w[np.clip(d + GAUSS_R, 0, 2 * GAUSS_R)], 0.0).astype(np.float32)
    m = np.kron(np.eye(planes, dtype=np.float32), m)
    hi, lo = split2(m)
    return np.concatenate([hi, hi, lo], axis=1)


def suffix_prefix(first, second):
    n = len(first)
    suf = [None] * n
    suf[n - 1] = first[n - 1]
    for i in range(n - 2, -1, -1):
        suf[i] = first[i] + suf[i + 1]
    out = []
    run = None
    for i in range(n):
        run = second[i] if run is None else run + second[i]
        out.append(suf[i] + run)
    return out


PEERS = ((0, 0), (1, 2), (0, 2), (1, 1), (1, 3), (0, 1), (0, 3), (1, 0))
VM = pl.BlockSpec(memory_space=pltpu.VMEM)
SM = pl.BlockSpec(memory_space=pltpu.SMEM)
HB = pl.BlockSpec(memory_space=pltpu.HBM)


def peer(s, dz, dy):
    return (s & 4) ^ (4 * dz) | ((s + dy) & 3)


def params():
    return pltpu.CompilerParams(vmem_limit_bytes=20 * 1024 * 1024)


def volume(planes, rows=64):
    return jax.ShapeDtypeStruct((planes, rows, 256), F32)


def pack_kernel(me, src, full, head, tail, *rest):
    pieces, (stage, sem) = rest[:-2], rest[-2:]
    idx = [pl.multiple_of(peer(me[0], dz, dy) * 8, 8) for dz, dy in PEERS]
    n = src.shape[0] // BZ
    copies = [
        [
            pltpu.make_async_copy(
                src.at[pl.ds(BZ * b, BZ), :, pl.ds(128 * h, 128)], stage.at[h, pl.ds(BZ * b, BZ)], sem.at[b, h])
            for h in range(2)
        ]
        for b in range(n)
    ]
    for pair in copies:
        for copy in pair:
            copy.start()

    def body(p, c):
        for i in range(8):
            for h in range(2):
                full[p, pl.ds(8 * i, 8), pl.ds(128 * h, 128)] = stage[h, p, pl.ds(i, 8, stride=8), :]
        return c

    def cut(p, c):
        for ref, row in zip(pieces, idx):
            ref[p] = full[p, pl.ds(row, 8), :]
        return c
    for b in range(n):
        for copy in copies[b]:
            copy.wait()
        lax.fori_loop(BZ * b, BZ * (b + 1), body, 0)
        lax.fori_loop(BZ * b, BZ * (b + 1), cut, 0)
    head[...] = full[:BOX_R]
    tail[...] = full[BZ * n - BOX_R:]


def pack_call(me, moving):
    planes = moving.shape[0]
    return pl.pallas_call(
        pack_kernel,
        name="pack",
        in_specs=[SM, HB],
        out_specs=[VM] * (3 + len(PEERS)),
        out_shape=[volume(planes), volume(BOX_R), volume(BOX_R)] + [volume(planes, 8)] * len(PEERS),
        scratch_shapes=[pltpu.VMEM((2, planes, 64, 128), F32), pltpu.SemaphoreType.DMA((planes // BZ, 2))],
        compiler_params=params(),
    )(me, moving)


def gather_kernel(me, *refs):
    n = len(PEERS)
    pieces, (full, head, tail) = refs[:n], refs[n:]
    idx = [pl.multiple_of(peer(me[0], dz, dy) * 8, 8) for dz, dy in PEERS]

    def body(p, c):
        for piece, row in zip(pieces, idx):
            full[p, pl.ds(row, 8), :] = piece[p]
        return c
    planes = full.shape[0]
    lax.fori_loop(0, planes, body, 0)
    head[...] = full[:BOX_R]
    tail[...] = full[planes - BOX_R:]


def gather_call(me, pieces):
    planes = pieces[0].shape[0]
    return pl.pallas_call(
        gather_kernel,
        name="gather",
        in_specs=[SM] + [VM] * len(pieces),
        out_specs=[VM] * 3,
        out_shape=[volume(planes), volume(BOX_R), volume(BOX_R)],
        compiler_params=params(),
    )(me, *pieces)


def natural_kernel(src, dst, stage, out, sem):
    n = src.shape[0] // BZ

    def fill(p, c):
        for h in range(2):
            stage[p, h] = src[p, :, pl.ds(128 * h, 128)]
        return c

    def body(p, c):
        for h in range(2):
            for i in range(8):
                out[p, pl.ds(8 * i, 8), pl.ds(128 * h, 128)] = stage[p, h, pl.ds(i, 8, stride=8), :]
        return c
    copies = []
    for b in range(n):
        lax.fori_loop(BZ * b, BZ * (b + 1), fill, 0)
        lax.fori_loop(BZ * b, BZ * (b + 1), body, 0)
        block = pl.ds(BZ * b, BZ)
        copies.append(pltpu.make_async_copy(out.at[block], dst.at[block], sem.at[b]))
        copies[-1].start()
    for copy in copies:
        copy.wait()


def natural_call(array):
    planes = array.shape[0]
    return pl.pallas_call(
        natural_kernel,
        name="natural",
        in_specs=[VM],
        out_specs=HB,
        out_shape=volume(planes),
        scratch_shapes=[
            pltpu.VMEM((planes, 2, 64, 128), F32),
            pltpu.VMEM((planes, 64, 256), F32),
            pltpu.SemaphoreType.DMA((planes // BZ,)),
        ],
        compiler_params=params(),
    )(array)


def edge_sums(items):
    core = items[3]
    for v in items[4:9]:
        core = core + v
    s2, p9 = items[2], items[9]
    s1 = items[1] + s2
    p10 = p9 + items[10]
    return [items[0] + s1 + core, s1 + core + p9, s2 + core + p10, core + (p10 + items[11])]


def z_loop(out, terms, get):
    def body(q, c):
        rows = pl.ds(pl.multiple_of(q * 8, 8), 8)
        for h in range(2):
            cols = pl.ds(128 * h, 128)
            one, two = get(rows, cols)
            for ref, term in zip(out, terms):
                a, b = [term(v) for v in one], [term(v) for v in two]
                res = suffix_prefix(a, b) if len(a) == 8 else edge_sums(a) + edge_sums(b)
                for p in range(8):
                    ref[p, rows, cols] = res[p]
        return c
    lax.fori_loop(0, 8, body, 0)


def y_sums_split(ref, parts):
    sub = lax.broadcasted_iota(jnp.int32, (8, 128), 0)
    first_row, last_row = sub == 0, sub == 7

    def body(p, c):
        for h in range(2):
            cols = pl.ds(128 * h, 128)
            x = [ref[p, pl.ds(8 * i, 8), cols] for i in range(8)]
            down = [jnp.where(first_row, 0.0, pltpu.roll(x[i], 1, 0)) for i in range(4, 8)]
            up = [jnp.where(last_row, 0.0, pltpu.roll(x[i], 7, 0)) for i in range(4)]
            res = suffix_prefix(down + x[:4], x[4:] + up)
            for j in range(4):
                v = jnp.concatenate([res[2 * j], res[2 * j + 1]], axis=0)
                hi = v.astype(BF16)
                v = v - hi.astype(F32)
                mid = v.astype(BF16)
                lo = (v - mid.astype(F32)).astype(BF16)
                rows = pl.ds(pl.multiple_of(p * 64, 64) + 16 * j, 16)
                parts[rows, pl.ds(128 * h, 128)] = hi
                parts[rows, pl.ds(256 + 128 * h, 128)] = mid
                parts[rows, pl.ds(512 + 128 * h, 128)] = lo
        return c
    lax.fori_loop(0, 8, body, 0)


def x_sums(parts, band, out):
    out[...] = jnp.dot(parts[...], band[...], preferred_element_type=F32).reshape(out.shape)


def mid_planes(ref, j):
    return lambda r, c: ([ref[8 * j + p, r, c] for p in range(8)], [ref[8 * j + 8 + p, r, c] for p in range(8)])


def edge_planes(lo, ref, hi):
    n = ref.shape[0]
    return lambda r, c: (
        [lo[p, r, c] for p in range(4)] + [ref[p, r, c] for p in range(8)],
        [ref[n - 8 + p, r, c] for p in range(8)] + [hi[p, r, c] for p in range(4)],
    )


def both(get_a, get_b):
    def get(r, c):
        a, b = get_a(r, c), get_b(r, c)
        return tuple(list(zip(x, y)) for x, y in zip(a, b))
    return get


def moving_block(get, band, mean, var, at, zs, parts, sums):
    z_loop([zs.at[0], zs.at[1]], [lambda a: a, lambda a: a * a], get)
    for v in range(2):
        y_sums_split(zs.at[v], parts)
        x_sums(parts, band, sums.at[v])

    def point(p, c):
        m = sums[0, p] * INV
        mean[at + p] = m
        var[at + p] = sums[1, p] * INV - m * m
        return c
    lax.fori_loop(0, 8, point, 0)


def moving_mid_kernel(ip, band, mean, var, zs, parts, sums):
    def step(j, c):
        moving_block(mid_planes(ip, j), band, mean, var, 8 * j, zs, parts, sums)
        return c
    lax.fori_loop(0, mean.shape[0] // BZ, step, 0)


def moving_edge_kernel(lo, ip, hi, band, mean, var, zs, parts, sums):
    moving_block(edge_planes(lo, ip, hi), band, mean, var, 0, zs, parts, sums)


def box_scratch(v):
    return [
        pltpu.VMEM((v, BZ, 64, 256), F32),
        pltpu.VMEM((BZ * 64, 768), BF16),
        pltpu.VMEM((v, BZ, 64, 256), F32),
    ]


def moving_call(*images):
    planes = images[0].shape[0] - BZ if len(images) == 1 else BZ
    return pl.pallas_call(
        moving_mid_kernel if len(images) == 1 else moving_edge_kernel,
        name="moving",
        in_specs=[VM] * (len(images) + 1),
        out_specs=[VM] * 2,
        out_shape=[volume(planes)] * 2,
        scratch_shapes=box_scratch(2),
        compiler_params=params(),
    )(*images, jnp.asarray(band_ones(256), BF16))


def factor_block(get_t, get_i, cell_t, cell_i, mean, var, at, band, fac, loss, zs, parts, sums):
    z_loop([zs.at[0], zs.at[1]], [lambda a: a, lambda a: a * a], get_t)
    z_loop([zs.at[2]], [lambda a: a[0] * a[1]], both(get_t, get_i))
    for v in range(3):
        y_sums_split(zs.at[v], parts)
        x_sums(parts, band, sums.at[v])

    def point(t, c):
        p = t >> 2
        rows = pl.ds(pl.multiple_of((t & 3) * 16, 16), 16)
        j0 = cell_t(p, rows)
        i0 = cell_i(p, rows)
        mj = sums[0, p, rows, :] * INV
        vj = sums[1, p, rows, :] * INV - mj * mj
        mi = mean[at + p, rows, :]
        vi = var[at + p, rows, :]
        cc = sums[2, p, rows, :] * INV - mi * mj
        e = cc / (vi * vj + epsilon)
        fac[at + p, rows, :] = e * ((j0 - mj) - cc / (vi + epsilon) * (i0 - mi))
        loss[...] += cc * e
        return c
    lax.fori_loop(0, 32, point, 0)


def factor_mid_kernel(t, ip, mean, var, band, fac, total, zs, parts, sums, loss):
    loss[...] = jnp.zeros(loss.shape, F32)

    def step(j, c):
        cell = lambda ref: lambda p, rows: ref[8 * j + 4 + p, rows, :]
        factor_block(mid_planes(t, j), mid_planes(ip, j), cell(t), cell(ip), mean, var, 8 * j, band, fac, loss,
                     zs, parts, sums)
        return c
    lax.fori_loop(0, fac.shape[0] // BZ, step, 0)
    total[0] = jnp.sum(loss[...])


def factor_edge_kernel(tlo, t, thi, ilo, ip, ihi, mean, var, before, band, fac, first, last, total, zs, parts, sums, loss):
    loss[...] = jnp.zeros(loss.shape, F32)
    n = t.shape[0]
    cell = lambda ref: lambda p, rows: ref[jnp.where(p < 4, p, n - 8 + p), rows, :]
    factor_block(edge_planes(tlo, t, thi), edge_planes(ilo, ip, ihi), cell(t), cell(ip), mean, var, 0, band, fac, loss,
                 zs, parts, sums)
    first[...] = fac[:GAUSS_R]
    last[...] = fac[BZ - GAUSS_R:]
    total[0] = before[0] + jnp.sum(loss[...])


def factor_mid_call(target, full, mean, var):
    return pl.pallas_call(
        factor_mid_kernel,
        name="factor",
        in_specs=[VM] * 5,
        out_specs=[VM, SM],
        out_shape=[volume(mean.shape[0]), jax.ShapeDtypeStruct((1,), F32)],
        scratch_shapes=box_scratch(3) + [pltpu.VMEM((16, 256), F32)],
        compiler_params=params(),
    )(target, full, mean, var, jnp.asarray(band_ones(256), BF16))


def factor_edge_call(tlo, target, thi, ilo, full, ihi, mean, var, total):
    return pl.pallas_call(
        factor_edge_kernel,
        name="factor_edge",
        in_specs=[VM] * 8 + [SM, VM],
        out_specs=[VM] * 3 + [SM],
        out_shape=[volume(BZ), volume(GAUSS_R), volume(GAUSS_R), jax.ShapeDtypeStruct((1,), F32)],
        scratch_shapes=box_scratch(3) + [pltpu.VMEM((16, 256), F32)],
        compiler_params=params(),
    )(tlo, target, thi, ilo, full, ihi, mean, var, total, jnp.asarray(band_ones(256), BF16))


def raw_planes(comp, n, fac_at, image_at, raw):
    sub = lax.broadcasted_iota(jnp.int32, (8, 128), 0)
    lane = lax.broadcasted_iota(jnp.int32, (8, 128), 1)

    def body(q, c):
        mid = image_at(q)
        for i in range(8):
            rows = pl.ds(8 * i, 8)
            if comp == 2:
                im = [mid(rows, pl.ds(128 * h, 128)) for h in range(2)]
                left = [pltpu.roll(v, 127, 1) for v in im]
                right = [pltpu.roll(v, 1, 1) for v in im]
                e, s = lane == 127, lane == 0
                up = [jnp.where(e, left[1], left[0]), jnp.where(e, 0.0, left[1])]
                dn = [jnp.where(s, 0.0, right[0]), jnp.where(s, right[0], right[1])]
            for h in range(2):
                cols = pl.ds(128 * h, 128)
                if comp == 0:
                    slope = image_at(q + 1)(rows, cols) - image_at(q - 1)(rows, cols)
                elif comp == 1:
                    u = mid(pl.ds(8 * ((i + 1) % 8), 8), cols)
                    d = mid(pl.ds(8 * ((i + 7) % 8), 8), cols)
                    u = jnp.where(sub == 7, 0.0, pltpu.roll(u, 7, 0)) if i == 7 else u
                    d = jnp.where(sub == 0, 0.0, pltpu.roll(d, 1, 0)) if i == 0 else d
                    slope = u - d
                else:
                    slope = up[h] - dn[h]
                raw[q, rows, cols] = fac_at(q)(rows, cols) * slope
        return c
    lax.fori_loop(0, n, body, 0)


def blur_block(raw, at, ax, ay, out, xp, xs, yp):
    w = [float(v) for v in blur_weights()]

    def z_pass(q, c):
        top = pl.multiple_of(q * 16, 16)
        rows = pl.ds(top, 16)
        for h in range(2):
            cols = pl.ds(128 * h, 128)
            x = [raw[at + p, rows, cols] for p in range(14)]
            for p in range(8):
                v = w[3] * x[p + 3]
                for d in range(1, 4):
                    v = v + w[3 - d] * (x[p + 3 - d] + x[p + 3 + d])
                hi = v.astype(BF16)
                lo = (v - hi.astype(F32)).astype(BF16)
                dst = pl.ds(64 * p + top, 16)
                xp[dst, pl.ds(128 * h, 128)] = hi
                xp[dst, pl.ds(256 + 128 * h, 128)] = lo
                xp[dst, pl.ds(512 + 128 * h, 128)] = hi
        return c
    lax.fori_loop(0, 4, z_pass, 0)
    xs[...] = jnp.dot(xp[...], ax[...], preferred_element_type=F32)

    def split(t, c):
        rows = pl.ds(pl.multiple_of(t * 32, 32), 32)
        v = xs[rows, :]
        hi = v.astype(BF16)
        g = t >> 3
        r = pl.multiple_of((t & 7) * 32, 32)
        yp[g, pl.ds(r, 32), :] = hi
        yp[g, pl.ds(256 + r, 32), :] = (v - hi.astype(F32)).astype(BF16)
        yp[g, pl.ds(512 + r, 32), :] = hi
        return c
    lax.fori_loop(0, 16, split, 0)
    for g in range(2):
        out[pl.ds(4 * g, 4)] = jnp.dot(ay[...], yp[g], preferred_element_type=F32).reshape(4, 64, 256)


def at_plane(ref):
    return lambda q: lambda r, c: ref[q, r, c]


def blur_mid_kernel(comp, fac, ip, ax, ay, *rest):
    force, raw, out, xp, xs, yp, sem = rest[-7:]
    n = fac.shape[0]
    raw_planes(comp, n, at_plane(fac), lambda q: at_plane(ip)(q + 4), raw)
    copies = []
    for m in range(n // BZ - 1):
        blur_block(raw, BZ * m + 1, ax, ay, out.at[m], xp, xs, yp)
        copies.append(pltpu.make_async_copy(out.at[m], force.at[comp, pl.ds(BZ * (m + 1), BZ)], sem.at[m]))
        copies[-1].start()
    for copy in copies:
        copy.wait()


def blur_edge_kernel(facm, face, flo, fhi, ilo, ip, ihi, ax, ay, before, force, image, fac, raw, out, xp, xs, yp, sem):
    n = ip.shape[0]
    m = facm.shape[0]
    copies = []
    for side in range(2):
        if side == 0:
            image[:4] = ilo[...]
            image[4:20] = ip[:16]
            fac[:3] = flo[...]
            fac[3:7] = face[:4]
            fac[7:14] = facm[:7]
        else:
            image[:16] = ip[n - 16:]
            image[16:20] = ihi[...]
            fac[:7] = facm[m - 7:]
            fac[7:11] = face[4:]
            fac[11:14] = fhi[...]
        shift = 1 if side == 0 else 5
        for comp in range(3):
            raw_planes(comp, 14, at_plane(fac), lambda q: at_plane(image)(q + shift), raw)
            slot = 3 * side + comp
            blur_block(raw, 0, ax, ay, out.at[slot], xp, xs, yp)
            copies.append(pltpu.make_async_copy(
                out.at[slot], force.at[comp, pl.ds(0 if side == 0 else n - BZ, BZ)], sem.at[slot]))
            copies[-1].start()
    for copy in copies:
        copy.wait()


def blur_scratch(planes, blocks):
    return [
        pltpu.VMEM((planes, 64, 256), F32),
        pltpu.VMEM((blocks, BZ, 64, 256), F32),
        pltpu.VMEM((BZ * 64, 768), BF16),
        pltpu.VMEM((BZ * 64, 256), F32),
        pltpu.VMEM((2, 768, 256), BF16),
        pltpu.SemaphoreType.DMA((blocks,)),
    ]


def blur_mid_call(comp, fac, full, force):
    n = fac.shape[0]
    kept = [] if force is None else [force]
    return pl.pallas_call(
        functools.partial(blur_mid_kernel, comp),
        name="blur",
        in_specs=[VM] * 4 + [HB] * len(kept),
        out_specs=HB,
        out_shape=jax.ShapeDtypeStruct((3,) + full.shape, F32),
        input_output_aliases={4: 0} if kept else {},
        scratch_shapes=blur_scratch(n, n // BZ - 1),
        compiler_params=params(),
    )(fac, full, jnp.asarray(gauss_x(256), BF16), jnp.asarray(gauss_y(64, 4), BF16), *kept)


def blur_edge_call(facm, face, flo, fhi, ilo, full, ihi, force):
    return pl.pallas_call(
        blur_edge_kernel,
        name="blur_edge",
        in_specs=[VM] * 9 + [HB],
        out_specs=HB,
        out_shape=jax.ShapeDtypeStruct((3,) + full.shape, F32),
        input_output_aliases={9: 0},
        scratch_shapes=[pltpu.VMEM((20, 64, 256), F32), pltpu.VMEM((14, 64, 256), F32)] + blur_scratch(14, 6),
        compiler_params=params(),
    )(facm, face, flo, fhi, ilo, full, ihi, jnp.asarray(gauss_x(256), BF16), jnp.asarray(gauss_y(64, 4), BF16), force)


from jax.sharding import PartitionSpec as P


def halo(first, last, size):
    up = [(i, i + 1) for i in range(size - 1)]
    down = [(j, i) for i, j in up]
    return lax.ppermute(last, "gz", up), lax.ppermute(first, "gz", down)


def steps(warped):
    moving = warped[0]
    planes = moving.shape[0]
    size = lax.axis_size("gz")
    me = jnp.reshape(lax.axis_index("subj"), (1,)).astype(jnp.int32)
    pairs = [[(i, peer(i, dz, dy)) for i in range(8)] for dz, dy in PEERS]
    back = [[(b, a) for a, b in pair] for pair in pairs]

    full, head, tail, *pieces = pack_call(me, moving)
    got = [lax.ppermute(pieces[j], "subj", pairs[j]) for j in range(1, 8)]
    ilo, ihi = halo(head, tail, size)
    mean, var = moving_call(full)
    own = pieces[0]
    for piece in got:
        own = own + piece
    own = own * 0.125
    got = [own] + [lax.ppermute(own, "subj", back[j]) for j in range(1, 8)]
    mean_e, var_e = moving_call(ilo, full, ihi)
    target, thead, ttail = gather_call(me, got)
    tlo, thi = halo(thead, ttail, size)
    fac, total = factor_mid_call(target, full, mean, var)
    fac_e, first, last, total = factor_edge_call(tlo, target, thi, ilo, full, ihi, mean_e, var_e, total)
    flo, fhi = halo(first, last, size)
    force = None
    for n, step in enumerate((1, 2, 4, 8)):
        other = lax.ppermute(total, "gz", [(i, i ^ step) for i in range(size)])
        if n < 3:
            force = blur_mid_call(n, fac, full, force)
        else:
            force = blur_edge_call(fac, fac_e, flo, fhi, ilo, full, ihi, force)
        total = total + other
    cells = float(size * planes * moving.shape[1] * moving.shape[2])
    template = natural_call(target)
    return force[None], template, -total / cells


def solution(mesh):
    return jax.shard_map(
        steps,
        mesh=mesh,
        in_specs=(P("subj", "gz", None, None),),
        out_specs=(P("subj", None, "gz", None, None), P("gz", None, None), P("subj")),
        check_vma=False,
    )
```

time: 340 us -> 161 us (0.47)
  other arithmetic: 175 us -> 0.14 us
  Pallas kernels: 0 us -> 57.4 us
  waiting for transfers between devices: 93.6 us -> 38.8 us
  starting transfers between devices: 15.5 us -> 56.4 us
  blocking collectives: 38.3 us -> 0 us
  between operations: 16 us -> 5.19 us
    psum x1 -> x0, waiting for transfers between devices: 87.4 us -> none  [on_device(): template = lax.psum(moving, 'subj') / members]
    add x9 -> x0, other arithmetic: 80.1 us -> none  [the longest x7 42.9 us: shifted_sum(): running + lax.slice_in_dim(padded, offset, offset + planes_out, axis=along)]
    pallas_call x0 -> x11, Pallas kernels: none -> 57.4 us  [the longest x3 15.1 us: blur_mid_call(): pl.pallas_call(functools.partial(blur_mid_kernel, comp), name='blur', in_...]
    ppermute x4 -> x24, starting transfers between devices: 15.5 us -> 56.4 us  [the longest x4 20.7 us: steps(): other = lax.ppermute(total, 'gz', [(i, i ^ step) for i in range(size)])]
    reduce_sum x1 -> x0, other arithmetic: 40.5 us -> none  [on_device(): loss = -lax.psum(jnp.sum(similarity), 'gz') / cells]
    psum x1 -> x0, blocking collectives: 38.3 us -> none  [on_device(): loss = -lax.psum(jnp.sum(similarity), 'gz') / cells]
    ppermute x4 -> x24, waiting for transfers between devices: 5.57 us -> 38.8 us  [the longest x7 19.8 us: steps(): got = [lax.ppermute(pieces[j], 'subj', pairs[j]) for j in range(1, 8)]]
    broadcast_in_dim x1 -> x0, other arithmetic: 25.3 us -> none  [on_device(): return (smoothed[None], template, jnp.reshape(loss, (1,)))]
  transfers between devices with their start and end apart: 5 -> 24, of which waited for: 3 -> 15; matrix products, arithmetic and copies ran while one was open for 0% -> 0% of each run, Pallas kernels for 0% -> 23%
where the time goes in v2:
time: 161 us; the launch traced here: 160 us
  Pallas kernels  57.4 us (36%)
  starting transfers between devices  56.4 us (35%)
  waiting for transfers between devices  38.8 us (24%)
  between operations  5.19 us (3%)
    ppermute x4, starting transfers between devices, steps(): other = lax.ppermute(total, 'gz', [(i, i ^ step) for i in range(size)])  20.7 us
    ppermute x7, waiting for transfers between devices, steps(): got = [lax.ppermute(pieces[j], 'subj', pairs[j]) for j in range(1, 8)]  19.8 us
    ppermute x7, waiting for transfers between devices, steps(): got = [own] + [lax.ppermute(own, 'subj', back[j]) for j in range(1, 8)]  17.5 us
    pallas_call x3, Pallas kernels, blur_mid_call(): pl.pallas_call(functools.partial(blur_mid_kernel, comp), name='blur', in_...  15.1 us
    pallas_call x1, Pallas kernels, blur_edge_call(): pl.pallas_call(blur_edge_kernel, name='blur_edge', in_specs=[VM] * 9 + [H...  14.2 us
    ppermute x7, starting transfers between devices, steps(): got = [lax.ppermute(pieces[j], 'subj', pairs[j]) for j in range(1, 8)]  12.7 us
    ppermute x7, starting transfers between devices, steps(): got = [own] + [lax.ppermute(own, 'subj', back[j]) for j in range(1, 8)]  11.8 us
    pallas_call x1, Pallas kernels, factor_mid_call(): pl.pallas_call(factor_mid_kernel, name='factor', in_specs=[VM] * 5, out_s...  11.3 us
  transfers between devices with their start and end apart: 24, of which 15 were waited for; matrix products, arithmetic and copies ran while one was open for 0% of the time, Pallas kernels for 23%

profile of v2, /device:TPU:0, one launch (start us, length us, event | category | flops | bytes accessed | tf_op | source)
XLA Modules:
  0.0 159.6 jit_solution(2668933497810571795)
XLA Ops:
  0.6 1.6 copy-done.3
  3.5 4.7 %collective-permute-start = (f32[32,8,256]{2,1,0:T(8,128)S(1)}, f32[32,8,256]{2,1,0:T(8,128)S(1)}, u32[]{:S(2)}, u32[]{:S(2)}) collective-permute-start(f32[32,8,256]{2,1,0:T(8,128)S(1)} %get-tuple-element.28), channel_id=1, source_target_pairs={{0,96},{16,112},{32,64},{48,80},{64,32},{80,48},{96,0},{112,16},{1... | collective-permute-start | bytes 786440 | tf_op jit(solution)/shard_map/ppermute | solution.py:571
  9.7 3.0 %collective-permute-start.3 = (f32[32,8,256]{2,1,0:T(8,128)S(1)}, f32[32,8,256]{2,1,0:T(8,128)S(1)}, u32[]{:S(2)}, u32[]{:S(2)}) collective-permute-start(f32[32,8,256]{2,1,0:T(8,128)S(1)} %get-tuple-element.31), channel_id=1, source_target_pairs={{0,112},{16,64},{32,80},{48,96},{64,48},{80,0},{96,16},{112,32},{1... | collective-permute-start | bytes 786440 | tf_op jit(solution)/shard_map/ppermute | solution.py:571
  13.0 2.4 %collective-permute-done = f32[32,8,256]{2,1,0:T(8,128)S(1)} collective-permute-done((f32[32,8,256]{2,1,0:T(8,128)S(1)}, f32[32,8,256]{2,1,0:T(8,128)S(1)}, u32[]{:S(2)}, u32[]{:S(2)}) %collective-permute-start) | collective-permute-done | bytes 262176 | tf_op jit(solution)/shard_map/ppermute | solution.py:571
  15.4 2.9 %collective-permute-start.5 = (f32[32,8,256]{2,1,0:T(8,128)S(1)}, f32[32,8,256]{2,1,0:T(8,128)S(1)}, u32[]{:S(2)}, u32[]{:S(2)}) collective-permute-start(f32[32,8,256]{2,1,0:T(8,128)S(1)} %get-tuple-element.33), channel_id=1, source_target_pairs={{0,48},{16,0},{32,16},{48,32},{64,112},{80,64},{96,80},{112,96},{1... | collective-permute-start | bytes 786440 | tf_op jit(solution)/shard_map/ppermute | solution.py:571
  18.3 3.0 %collective-permute-done.1 = f32[32,8,256]{2,1,0:T(8,128)S(1)} collective-permute-done((f32[32,8,256]{2,1,0:T(8,128)S(1)}, f32[32,8,256]{2,1,0:T(8,128)S(1)}, u32[]{:S(2)}, u32[]{:S(2)}) %collective-permute-start.1) | collective-permute-done | bytes 262176 | tf_op jit(solution)/shard_map/ppermute | solution.py:571
  21.6 7.5 %collective-permute-done.2 = f32[32,8,256]{2,1,0:T(8,128)S(1)} collective-permute-done((f32[32,8,256]{2,1,0:T(8,128)S(1)}, f32[32,8,256]{2,1,0:T(8,128)S(1)}, u32[]{:S(2)}, u32[]{:S(2)}) %collective-permute-start.2) | collective-permute-done | bytes 262176 | tf_op jit(solution)/shard_map/ppermute | solution.py:571
  29.1 1.6 %collective-permute-done.3 = f32[32,8,256]{2,1,0:T(8,128)S(1)} collective-permute-done((f32[32,8,256]{2,1,0:T(8,128)S(1)}, f32[32,8,256]{2,1,0:T(8,128)S(1)}, u32[]{:S(2)}, u32[]{:S(2)}) %collective-permute-start.3) | collective-permute-done | bytes 262176 | tf_op jit(solution)/shard_map/ppermute | solution.py:571
  30.7 2.4 %collective-permute-done.4 = f32[32,8,256]{2,1,0:T(8,128)S(1)} collective-permute-done((f32[32,8,256]{2,1,0:T(8,128)S(1)}, f32[32,8,256]{2,1,0:T(8,128)S(1)}, u32[]{:S(2)}, u32[]{:S(2)}) %collective-permute-start.4) | collective-permute-done | bytes 262176 | tf_op jit(solution)/shard_map/ppermute | solution.py:571
  33.1 2.5 %collective-permute-done.5 = f32[32,8,256]{2,1,0:T(8,128)S(1)} collective-permute-done((f32[32,8,256]{2,1,0:T(8,128)S(1)}, f32[32,8,256]{2,1,0:T(8,128)S(1)}, u32[]{:S(2)}, u32[]{:S(2)}) %collective-permute-start.5) | collective-permute-done | bytes 262176 | tf_op jit(solution)/shard_map/ppermute | solution.py:571
  36.1 1.7 %collective-permute-start.13 = (f32[32,8,256]{2,1,0:T(8,128)S(1)}, f32[32,8,256]{2,1,0:T(8,128)S(1)}, u32[]{:S(2)}, u32[]{:S(2)}) collective-permute-start(f32[32,8,256]{2,1,0:T(8,128)S(1)} %add_multiply_fusion.refs_0_), channel_id=1, source_target_pairs={{64,0},{80,16},{96,32},{112,48},{0,64},{16,80},{32,96},{48,112},{6... | collective-permute-start | bytes 786440 | tf_op jit(solution)/shard_map/ppermute | solution.py:578
  39.2 1.8 %collective-permute-start.11 = (f32[32,8,256]{2,1,0:T(8,128)S(1)}, f32[32,8,256]{2,1,0:T(8,128)S(1)}, u32[]{:S(2)}, u32[]{:S(2)}) collective-permute-start(f32[32,8,256]{2,1,0:T(8,128)S(1)} %add_multiply_fusion.refs_0_), channel_id=1, source_target_pairs={{16,0},{32,16},{48,32},{0,48},{80,64},{96,80},{112,96},{64,112},{1... | collective-permute-start | bytes 786440 | tf_op jit(solution)/shard_map/ppermute | solution.py:578
  41.0 4.1 %collective-permute-start.9 = (f32[32,8,256]{2,1,0:T(8,128)S(1)}, f32[32,8,256]{2,1,0:T(8,128)S(1)}, u32[]{:S(2)}, u32[]{:S(2)}) collective-permute-start(f32[32,8,256]{2,1,0:T(8,128)S(1)} %add_multiply_fusion.refs_0_), channel_id=1, source_target_pairs={{80,0},{96,16},{112,32},{64,48},{16,64},{32,80},{48,96},{0,112},{8... | collective-permute-start | bytes 786440 | tf_op jit(solution)/shard_map/ppermute | solution.py:578
  45.1 1.7 %collective-permute-start.8 = (f32[32,8,256]{2,1,0:T(8,128)S(1)}, f32[32,8,256]{2,1,0:T(8,128)S(1)}, u32[]{:S(2)}, u32[]{:S(2)}) collective-permute-start(f32[32,8,256]{2,1,0:T(8,128)S(1)} %add_multiply_fusion.refs_0_), channel_id=1, source_target_pairs={{32,0},{48,16},{0,32},{16,48},{96,64},{112,80},{64,96},{80,112},{3... | collective-permute-start | bytes 786440 | tf_op jit(solution)/shard_map/ppermute | solution.py:578
  50.5 5.1 %collective-permute-done.10.refs_4_ = f32[32,8,256]{2,1,0:T(8,128)S(1)} collective-permute-done((f32[32,8,256]{2,1,0:T(8,128)S(1)}, f32[32,8,256]{2,1,0:T(8,128)S(1)}, u32[]{:S(2)}, u32[]{:S(2)}) %collective-permute-start.10) | collective-permute-done | bytes 262176 | tf_op jit(solution)/shard_map/ppermute | solution.py:578
  56.9 4.2 %collective-permute-done.8.refs_2_ = f32[32,8,256]{2,1,0:T(8,128)S(1)} collective-permute-done((f32[32,8,256]{2,1,0:T(8,128)S(1)}, f32[32,8,256]{2,1,0:T(8,128)S(1)}, u32[]{:S(2)}, u32[]{:S(2)}) %collective-permute-start.8) | collective-permute-done | bytes 262176 | tf_op jit(solution)/shard_map/ppermute | solution.py:578
  61.1 6.9 %collective-permute-done.7.refs_1_ = f32[32,8,256]{2,1,0:T(8,128)S(1)} collective-permute-done((f32[32,8,256]{2,1,0:T(8,128)S(1)}, f32[32,8,256]{2,1,0:T(8,128)S(1)}, u32[]{:S(2)}, u32[]{:S(2)}) %collective-permute-start.7) | collective-permute-done | bytes 262176 | tf_op jit(solution)/shard_map/ppermute | solution.py:578
  71.2 6.3 %moving.2 = (f32[24,64,256]{2,1,0:T(8,128)S(1)}, f32[24,64,256]{2,1,0:T(8,128)S(1)}) custom-call(f32[32,64,256]{2,1,0:T(8,128)S(1)} %get-tuple-element.36.ip, bf16[768,256]{1,0:T(8,128)(2,1)S(1)} %copy-done), custom_call_target="tpu_custom_call" | custom-call | tf_op jit(solution)/shard_map/moving/pallas_call | solution.py:316
  77.5 2.1 %moving.3 = (f32[8,64,256]{2,1,0:T(8,128)S(1)}, f32[8,64,256]{2,1,0:T(8,128)S(1)}) custom-call(f32[4,64,256]{2,1,0:T(8,128)S(1)} %collective-permute-done.16.lo.ilo, f32[32,64,256]{2,1,0:T(8,128)S(1)} %get-tuple-element.36.ip, f32[4,64,256]{2,1,0:T(8,128)S(1)} %collective-permute-done.17.hi.ihi, bf16[768,256]{1,0:T(8,128)(2,1)S(1)} %copy-done), custom_call_target="tpu_custom_call" | custom-call | tf_op jit(solution)/shard_map/moving/pallas_call | solution.py:316
  79.6 11.3 %factor.1 = (f32[24,64,256]{2,1,0:T(8,128)S(1)}, f32[1]{0:T(128)}) custom-call(f32[32,64,256]{2,1,0:T(8,128)S(1)} %get-tuple-element.35.t.src, f32[32,64,256]{2,1,0:T(8,128)S(1)} %get-tuple-element.36.ip, f32[24,64,256]{2,1,0:T(8,128)S(1)} %get-tuple-element.37.mean, f32[24,64,256]{2,1,0:T(8,128)S(1)} %get-tuple-element.38.var, bf16[768,256]{1,0:T(8,128)(2,1)S(1)} %copy-done), custom_call_target="tpu_custom_call" | custom-call | tf_op jit(solution)/shard_map/factor/pallas_call | solution.py:375
  91.0 5.0 %factor_edge.1 = (f32[8,64,256]{2,1,0:T(8,128)S(1)}, f32[3,64,256]{2,1,0:T(8,128)S(1)}, f32[3,64,256]{2,1,0:T(8,128)S(1)}, f32[1]{0:T(128)}) custom-call(f32[4,64,256]{2,1,0:T(8,128)S(1)} %collective-permute-done.14.tlo, f32[32,64,256]{2,1,0:T(8,128)S(1)} %get-tuple-element.35.t.src, f32[4,64,256]{2,1,0:T(8,128)S(1)} %collective-permute-done.15.thi, ...), custom_call_target="tpu_custom_call" | custom-call | tf_op jit(solution)/shard_map/factor_edge/pallas_call | solution.py:387
  96.0 4.4 %collective-permute-start.18 = (f32[3,64,256]{2,1,0:T(8,128)S(1)}, f32[3,64,256]{2,1,0:T(8,128)S(1)}, u32[]{:S(2)}, u32[]{:S(2)}) collective-permute-start(f32[3,64,256]{2,1,0:T(8,128)S(1)} %get-tuple-element.48), channel_id=1, source_target_pairs={{0,1},{1,2},{2,3},{3,4},{4,5},{5,6},{6,7},{7,8},{8,9},{9,10},{10,1... | collective-permute-start | bytes 589832 | tf_op jit(solution)/shard_map/ppermute | solution.py:559
  100.5 1.6 %collective-permute-start.19 = (f32[3,64,256]{2,1,0:T(8,128)S(1)}, f32[3,64,256]{2,1,0:T(8,128)S(1)}, u32[]{:S(2)}, u32[]{:S(2)}) collective-permute-start(f32[3,64,256]{2,1,0:T(8,128)S(1)} %get-tuple-element.49), channel_id=1, source_target_pairs={{1,0},{2,1},{3,2},{4,3},{5,4},{6,5},{7,6},{8,7},{9,8},{10,9},{11,1... | collective-permute-start | bytes 589832 | tf_op jit(solution)/shard_map/ppermute | solution.py:559
  102.1 1.6 natural.1
  103.7 4.3 %blur.3.rest_0_ = f32[3,32,64,256]{3,2,1,0:T(8,128)} custom-call(f32[24,64,256]{2,1,0:T(8,128)S(1)} %get-tuple-element.39.fac.facm, f32[32,64,256]{2,1,0:T(8,128)S(1)} %get-tuple-element.36.ip, bf16[768,256]{1,0:T(8,128)(2,1)S(1)} %copy-done.2, bf16[256,768]{1,0:T(8,128)(2,1)S(1)} %copy-done.1), custom_call_target="tpu_custom_call" | custom-call | tf_op jit(solution)/shard_map/blur/pallas_call | solution.py:528
  108.0 4.3 %blur.4.rest_0_ = f32[3,32,64,256]{3,2,1,0:T(8,128)} custom-call(f32[24,64,256]{2,1,0:T(8,128)S(1)} %get-tuple-element.39.fac.facm, f32[32,64,256]{2,1,0:T(8,128)S(1)} %get-tuple-element.36.ip, bf16[768,256]{1,0:T(8,128)(2,1)S(1)} %copy-done.2, bf16[256,768]{1,0:T(8,128)(2,1)S(1)} %copy-done.1, ...), custom_call_target="tpu_custom_call", output_to_operand_aliasing={{}: (4, {})} | custom-call | tf_op jit(solution)/shard_map/blur/pallas_call | solution.py:528
  112.4 6.5 %blur.5.before = f32[3,32,64,256]{3,2,1,0:T(8,128)} custom-call(f32[24,64,256]{2,1,0:T(8,128)S(1)} %get-tuple-element.39.fac.facm, f32[32,64,256]{2,1,0:T(8,128)S(1)} %get-tuple-element.36.ip, bf16[768,256]{1,0:T(8,128)(2,1)S(1)} %copy-done.2, bf16[256,768]{1,0:T(8,128)(2,1)S(1)} %copy-done.1, ...), custom_call_target="tpu_custom_call", output_to_operand_aliasing={{}: (4, {})} | custom-call | tf_op jit(solution)/shard_map/blur/pallas_call | solution.py:528
  118.9 3.9 %collective-permute-start.20 = (f32[1]{0:T(128)}, f32[1]{0:T(128)}, u32[]{:S(2)}, u32[]{:S(2)}) collective-permute-start(f32[1]{0:T(128)} %get-tuple-element.50), channel_id=1, source_target_pairs={{0,1},{1,0},{2,3},{3,2},{4,5},{5,4},{6,7},{7,6},{8,9},{9,8},{10,11... | collective-permute-start | bytes 20 | tf_op jit(solution)/shard_map/ppermute | solution.py:587
  124.9 5.6 %collective-permute-start.21 = (f32[1]{0:T(128)}, f32[1]{0:T(128)}, u32[]{:S(2)}, u32[]{:S(2)}) collective-permute-start(f32[1]{0:T(128)} %add.40), channel_id=1, source_target_pairs={{0,2},{1,3},{2,0},{3,1},{4,6},{5,7},{6,4},{7,5},{8,10},{9,11},{10,... | collective-permute-start | bytes 20 | tf_op jit(solution)/shard_map/ppermute | solution.py:587
  131.3 6.3 %collective-permute-start.22 = (f32[1]{0:T(128)}, f32[1]{0:T(128)}, u32[]{:S(2)}, u32[]{:S(2)}) collective-permute-start(f32[1]{0:T(128)} %add.41), channel_id=1, source_target_pairs={{0,4},{1,5},{2,6},{3,7},{4,0},{5,1},{6,2},{7,3},{8,12},{9,13},{10,... | collective-permute-start | bytes 20 | tf_op jit(solution)/shard_map/ppermute | solution.py:587
  138.5 4.9 %collective-permute-start.23 = (f32[1]{0:T(128)}, f32[1]{0:T(128)}, u32[]{:S(2)}, u32[]{:S(2)}) collective-permute-start(f32[1]{0:T(128)} %add.42), channel_id=1, source_target_pairs={{0,8},{1,9},{2,10},{3,11},{4,12},{5,13},{6,14},{7,15},{8,0},{9,1},... | collective-permute-start | bytes 20 | tf_op jit(solution)/shard_map/ppermute | solution.py:587
  144.3 14.2 %blur_edge.1 = f32[3,32,64,256]{3,2,1,0:T(8,128)} custom-call(f32[24,64,256]{2,1,0:T(8,128)S(1)} %get-tuple-element.39.fac.facm, f32[8,64,256]{2,1,0:T(8,128)S(1)} %get-tuple-element.47.face, f32[3,64,256]{2,1,0:T(8,128)S(1)} %collective-permute-done.18.flo, f32[3,64,256]{2,1,0:T(8,128)S(1)} %collective-permute-done.19.fhi, ...), custom_call_target="tpu_custom_call", output_to_operand_aliasing={{}: (9, {})} | custom-call | tf_op jit(solution)/shard_map/blur_edge/pallas_call | solution.py:541
  (36 shorter events, 14.9 us)
Async XLA Ops:
  0.6 1.6 copy-start.3
  3.5 12.0 %collective-permute-start = (f32[32,8,256]{2,1,0:T(8,128)S(1)}, f32[32,8,256]{2,1,0:T(8,128)S(1)}, u32[]{:S(2)}, u32[]{:S(2)}) collective-permute-start(f32[32,8,256]{2,1,0:T(8,128)S(1)} %get-tuple-element.28), channel_id=1, source_target_pairs={{0,96},{16,112},{32,64},{48,80},{64,32},{80,48},{96,0},{112,16},{1... | collective-permute-start | bytes 786440 | tf_op jit(solution)/shard_map/ppermute | solution.py:571
  8.2 13.1 %collective-permute-start.1 = (f32[32,8,256]{2,1,0:T(8,128)S(1)}, f32[32,8,256]{2,1,0:T(8,128)S(1)}, u32[]{:S(2)}, u32[]{:S(2)}) collective-permute-start(f32[32,8,256]{2,1,0:T(8,128)S(1)} %get-tuple-element.29), channel_id=1, source_target_pairs={{0,32},{16,48},{32,0},{48,16},{64,96},{80,112},{96,64},{112,80},{1... | collective-permute-start | bytes 786440 | tf_op jit(solution)/shard_map/ppermute | solution.py:571
  8.5 20.6 %collective-permute-start.2 = (f32[32,8,256]{2,1,0:T(8,128)S(1)}, f32[32,8,256]{2,1,0:T(8,128)S(1)}, u32[]{:S(2)}, u32[]{:S(2)}) collective-permute-start(f32[32,8,256]{2,1,0:T(8,128)S(1)} %get-tuple-element.30), channel_id=1, source_target_pairs={{0,80},{16,96},{32,112},{48,64},{64,16},{80,32},{96,48},{112,0},{1... | collective-permute-start | bytes 786440 | tf_op jit(solution)/shard_map/ppermute | solution.py:571
  9.7 21.1 %collective-permute-start.3 = (f32[32,8,256]{2,1,0:T(8,128)S(1)}, f32[32,8,256]{2,1,0:T(8,128)S(1)}, u32[]{:S(2)}, u32[]{:S(2)}) collective-permute-start(f32[32,8,256]{2,1,0:T(8,128)S(1)} %get-tuple-element.31), channel_id=1, source_target_pairs={{0,112},{16,64},{32,80},{48,96},{64,48},{80,0},{96,16},{112,32},{1... | collective-permute-start | bytes 786440 | tf_op jit(solution)/shard_map/ppermute | solution.py:571
  12.7 20.5 %collective-permute-start.4 = (f32[32,8,256]{2,1,0:T(8,128)S(1)}, f32[32,8,256]{2,1,0:T(8,128)S(1)}, u32[]{:S(2)}, u32[]{:S(2)}) collective-permute-start(f32[32,8,256]{2,1,0:T(8,128)S(1)} %get-tuple-element.32), channel_id=1, source_target_pairs={{0,16},{16,32},{32,48},{48,0},{64,80},{80,96},{96,112},{112,64},{1... | collective-permute-start | bytes 786440 | tf_op jit(solution)/shard_map/ppermute | solution.py:571
  15.4 20.2 %collective-permute-start.5 = (f32[32,8,256]{2,1,0:T(8,128)S(1)}, f32[32,8,256]{2,1,0:T(8,128)S(1)}, u32[]{:S(2)}, u32[]{:S(2)}) collective-permute-start(f32[32,8,256]{2,1,0:T(8,128)S(1)} %get-tuple-element.33), channel_id=1, source_target_pairs={{0,48},{16,0},{32,16},{48,32},{64,112},{80,64},{96,80},{112,96},{1... | collective-permute-start | bytes 786440 | tf_op jit(solution)/shard_map/ppermute | solution.py:571
  21.3 14.6 %collective-permute-start.6 = (f32[32,8,256]{2,1,0:T(8,128)S(1)}, f32[32,8,256]{2,1,0:T(8,128)S(1)}, u32[]{:S(2)}, u32[]{:S(2)}) collective-permute-start(f32[32,8,256]{2,1,0:T(8,128)S(1)} %get-tuple-element.34), channel_id=1, source_target_pairs={{0,64},{16,80},{32,96},{48,112},{64,0},{80,16},{96,32},{112,48},{1... | collective-permute-start | bytes 786440 | tf_op jit(solution)/shard_map/ppermute | solution.py:571
  35.9 35.3 %copy-start = (bf16[768,256]{1,0:T(8,128)(2,1)S(1)}, bf16[768,256]{1,0:T(8,128)(2,1)}, u32[]{:S(2)}) copy-start(bf16[768,256]{1,0:T(8,128)(2,1)} %constant.17.clone.band) | copy-start | bytes 1179652
  36.1 9.0 %collective-permute-start.13 = (f32[32,8,256]{2,1,0:T(8,128)S(1)}, f32[32,8,256]{2,1,0:T(8,128)S(1)}, u32[]{:S(2)}, u32[]{:S(2)}) collective-permute-start(f32[32,8,256]{2,1,0:T(8,128)S(1)} %add_multiply_fusion.refs_0_), channel_id=1, source_target_pairs={{64,0},{80,16},{96,32},{112,48},{0,64},{16,80},{32,96},{48,112},{6... | collective-permute-start | bytes 786440 | tf_op jit(solution)/shard_map/ppermute | solution.py:578
  37.7 10.4 %collective-permute-start.12 = (f32[32,8,256]{2,1,0:T(8,128)S(1)}, f32[32,8,256]{2,1,0:T(8,128)S(1)}, u32[]{:S(2)}, u32[]{:S(2)}) collective-permute-start(f32[32,8,256]{2,1,0:T(8,128)S(1)} %add_multiply_fusion.refs_0_), channel_id=1, source_target_pairs={{48,0},{0,16},{16,32},{32,48},{112,64},{64,80},{80,96},{96,112},{4... | collective-permute-start | bytes 786440 | tf_op jit(solution)/shard_map/ppermute | solution.py:578
  39.2 10.0 %collective-permute-start.11 = (f32[32,8,256]{2,1,0:T(8,128)S(1)}, f32[32,8,256]{2,1,0:T(8,128)S(1)}, u32[]{:S(2)}, u32[]{:S(2)}) collective-permute-start(f32[32,8,256]{2,1,0:T(8,128)S(1)} %add_multiply_fusion.refs_0_), channel_id=1, source_target_pairs={{16,0},{32,16},{48,32},{0,48},{80,64},{96,80},{112,96},{64,112},{1... | collective-permute-start | bytes 786440 | tf_op jit(solution)/shard_map/ppermute | solution.py:578
  41.0 14.6 %collective-permute-start.10 = (f32[32,8,256]{2,1,0:T(8,128)S(1)}, f32[32,8,256]{2,1,0:T(8,128)S(1)}, u32[]{:S(2)}, u32[]{:S(2)}) collective-permute-start(f32[32,8,256]{2,1,0:T(8,128)S(1)} %add_multiply_fusion.refs_0_), channel_id=1, source_target_pairs={{112,0},{64,16},{80,32},{96,48},{48,64},{0,80},{16,96},{32,112},{1... | collective-permute-start | bytes 786440 | tf_op jit(solution)/shard_map/ppermute | solution.py:578
  41.0 15.9 %collective-permute-start.9 = (f32[32,8,256]{2,1,0:T(8,128)S(1)}, f32[32,8,256]{2,1,0:T(8,128)S(1)}, u32[]{:S(2)}, u32[]{:S(2)}) collective-permute-start(f32[32,8,256]{2,1,0:T(8,128)S(1)} %add_multiply_fusion.refs_0_), channel_id=1, source_target_pairs={{80,0},{96,16},{112,32},{64,48},{16,64},{32,80},{48,96},{0,112},{8... | collective-permute-start | bytes 786440 | tf_op jit(solution)/shard_map/ppermute | solution.py:578
  45.1 16.0 %collective-permute-start.8 = (f32[32,8,256]{2,1,0:T(8,128)S(1)}, f32[32,8,256]{2,1,0:T(8,128)S(1)}, u32[]{:S(2)}, u32[]{:S(2)}) collective-permute-start(f32[32,8,256]{2,1,0:T(8,128)S(1)} %add_multiply_fusion.refs_0_), channel_id=1, source_target_pairs={{32,0},{48,16},{0,32},{16,48},{96,64},{112,80},{64,96},{80,112},{3... | collective-permute-start | bytes 786440 | tf_op jit(solution)/shard_map/ppermute | solution.py:578
  48.1 19.8 %collective-permute-start.7 = (f32[32,8,256]{2,1,0:T(8,128)S(1)}, f32[32,8,256]{2,1,0:T(8,128)S(1)}, u32[]{:S(2)}, u32[]{:S(2)}) collective-permute-start(f32[32,8,256]{2,1,0:T(8,128)S(1)} %add_multiply_fusion.refs_0_), channel_id=1, source_target_pairs={{96,0},{112,16},{64,32},{80,48},{32,64},{48,80},{0,96},{16,112},{9... | collective-permute-start | bytes 786440 | tf_op jit(solution)/shard_map/ppermute | solution.py:578
  49.2 28.3 %collective-permute-start.16 = (f32[4,64,256]{2,1,0:T(8,128)S(1)}, f32[4,64,256]{2,1,0:T(8,128)S(1)}, u32[]{:S(2)}, u32[]{:S(2)}) collective-permute-start(f32[4,64,256]{2,1,0:T(8,128)S(1)} %get-tuple-element.42), channel_id=1, source_target_pairs={{0,1},{1,2},{2,3},{3,4},{4,5},{5,6},{6,7},{7,8},{8,9},{9,10},{10,1... | collective-permute-start | bytes 786440 | tf_op jit(solution)/shard_map/ppermute | solution.py:559
  55.6 21.9 %collective-permute-start.17 = (f32[4,64,256]{2,1,0:T(8,128)S(1)}, f32[4,64,256]{2,1,0:T(8,128)S(1)}, u32[]{:S(2)}, u32[]{:S(2)}) collective-permute-start(f32[4,64,256]{2,1,0:T(8,128)S(1)} %get-tuple-element.43), channel_id=1, source_target_pairs={{1,0},{2,1},{3,2},{4,3},{5,4},{6,5},{7,6},{8,7},{9,8},{10,9},{11,1... | collective-permute-start | bytes 786440 | tf_op jit(solution)/shard_map/ppermute | solution.py:559
  68.6 22.4 %collective-permute-start.14 = (f32[4,64,256]{2,1,0:T(8,128)S(1)}, f32[4,64,256]{2,1,0:T(8,128)S(1)}, u32[]{:S(2)}, u32[]{:S(2)}) collective-permute-start(f32[4,64,256]{2,1,0:T(8,128)S(1)} %get-tuple-element.40), channel_id=1, source_target_pairs={{0,1},{1,2},{2,3},{3,4},{4,5},{5,6},{6,7},{7,8},{8,9},{9,10},{10,1... | collective-permute-start | bytes 786440 | tf_op jit(solution)/shard_map/ppermute | solution.py:559
  69.9 21.1 %collective-permute-start.15 = (f32[4,64,256]{2,1,0:T(8,128)S(1)}, f32[4,64,256]{2,1,0:T(8,128)S(1)}, u32[]{:S(2)}, u32[]{:S(2)}) collective-permute-start(f32[4,64,256]{2,1,0:T(8,128)S(1)} %get-tuple-element.41), channel_id=1, source_target_pairs={{1,0},{2,1},{3,2},{4,3},{5,4},{6,5},{7,6},{8,7},{9,8},{10,9},{11,1... | collective-permute-start | bytes 786440 | tf_op jit(solution)/shard_map/ppermute | solution.py:559
  96.0 48.2 %collective-permute-start.18 = (f32[3,64,256]{2,1,0:T(8,128)S(1)}, f32[3,64,256]{2,1,0:T(8,128)S(1)}, u32[]{:S(2)}, u32[]{:S(2)}) collective-permute-start(f32[3,64,256]{2,1,0:T(8,128)S(1)} %get-tuple-element.48), channel_id=1, source_target_pairs={{0,1},{1,2},{2,3},{3,4},{4,5},{5,6},{6,7},{7,8},{8,9},{9,10},{10,1... | collective-permute-start | bytes 589832 | tf_op jit(solution)/shard_map/ppermute | solution.py:559
  100.5 3.2 %copy-start.1 = (bf16[256,768]{1,0:T(8,128)(2,1)S(1)}, bf16[256,768]{1,0:T(8,128)(2,1)}, u32[]{:S(2)}) copy-start(bf16[256,768]{1,0:T(8,128)(2,1)} %constant.19.clone.ay) | copy-start | bytes 1179652
  100.5 3.2 %copy-start.2 = (bf16[768,256]{1,0:T(8,128)(2,1)S(1)}, bf16[768,256]{1,0:T(8,128)(2,1)}, u32[]{:S(2)}) copy-start(bf16[768,256]{1,0:T(8,128)(2,1)} %constant.18.clone.ax) | copy-start | bytes 1179652
  100.5 43.7 %collective-permute-start.19 = (f32[3,64,256]{2,1,0:T(8,128)S(1)}, f32[3,64,256]{2,1,0:T(8,128)S(1)}, u32[]{:S(2)}, u32[]{:S(2)}) collective-permute-start(f32[3,64,256]{2,1,0:T(8,128)S(1)} %get-tuple-element.49), channel_id=1, source_target_pairs={{1,0},{2,1},{3,2},{4,3},{5,4},{6,5},{7,6},{8,7},{9,8},{10,9},{11,1... | collective-permute-start | bytes 589832 | tf_op jit(solution)/shard_map/ppermute | solution.py:559
  118.9 4.8 %collective-permute-start.20 = (f32[1]{0:T(128)}, f32[1]{0:T(128)}, u32[]{:S(2)}, u32[]{:S(2)}) collective-permute-start(f32[1]{0:T(128)} %get-tuple-element.50), channel_id=1, source_target_pairs={{0,1},{1,0},{2,3},{3,2},{4,5},{5,4},{6,7},{7,6},{8,9},{9,8},{10,11... | collective-permute-start | bytes 20 | tf_op jit(solution)/shard_map/ppermute | solution.py:587
  124.9 5.8 %collective-permute-start.21 = (f32[1]{0:T(128)}, f32[1]{0:T(128)}, u32[]{:S(2)}, u32[]{:S(2)}) collective-permute-start(f32[1]{0:T(128)} %add.40), channel_id=1, source_target_pairs={{0,2},{1,3},{2,0},{3,1},{4,6},{5,7},{6,4},{7,5},{8,10},{9,11},{10,... | collective-permute-start | bytes 20 | tf_op jit(solution)/shard_map/ppermute | solution.py:587
  131.3 6.5 %collective-permute-start.22 = (f32[1]{0:T(128)}, f32[1]{0:T(128)}, u32[]{:S(2)}, u32[]{:S(2)}) collective-permute-start(f32[1]{0:T(128)} %add.41), channel_id=1, source_target_pairs={{0,4},{1,5},{2,6},{3,7},{4,0},{5,1},{6,2},{7,3},{8,12},{9,13},{10,... | collective-permute-start | bytes 20 | tf_op jit(solution)/shard_map/ppermute | solution.py:587
  138.5 5.1 %collective-permute-start.23 = (f32[1]{0:T(128)}, f32[1]{0:T(128)}, u32[]{:S(2)}, u32[]{:S(2)}) collective-permute-start(f32[1]{0:T(128)} %add.42), channel_id=1, source_target_pairs={{0,8},{1,9},{2,10},{3,11},{4,12},{5,13},{6,14},{7,15},{8,0},{9,1},... | collective-permute-start | bytes 20 | tf_op jit(solution)/shard_map/ppermute | solution.py:587
